TPU v7x, 32 devices: a whole 2x2x4 slice. The times are simulated.
32 devices in a mesh: slab: 8 (over y, x, core), group: 4 (over z).
Axes of the slice: x: 2, y: 2, z: 4, core: 2. Of those that a mesh axis runs over, the one named last changes fastest.
Arguments:
- disp_now: float32 [3, 262144], P(None, 'slab'), may hold values from -6 to 6
- disp_prev: float32 [3, 262144], P(None, 'slab'), may hold values from -6 to 6
- inv_mass: float32 [262144], P('slab'), may hold values from 0.5 to 2
- cell_nodes: int32 [1024, 192], P(('slab', 'group')), may hold values from 0 to 98303
- shape_grads: bfloat16 [1024, 3, 192, 128], P(('slab', 'group')), may hold values from -0.125 to 0.125
- cell_weights: float32 [1024, 128], P(('slab', 'group')), may hold values from 0.5 to 2
- cell_shear: float32 [1024], P(('slab', 'group')), may hold values from 0.5 to 2
- cell_bulk: float32 [1024], P(('slab', 'group')), may hold values from 1 to 4
- block_owner: int32 [1024, 1], P(('slab', 'group')), may hold values from 0 to 7; in each aligned block of 32 rows (0 to 31, 32 to 63, ...) at most 4 rows name the same one
- block_nodes: int32 [1024, 256], P(('slab', 'group')), may hold values from 0 to 32767
- block_phi: float32 [1024, 128, 256], P(('slab', 'group')), may hold values from -0.375 to 0.375
- block_corr: float32 [1024, 128, 128], P(('slab', 'group')), may hold values from -0.5 to 0.5
- block_target: float32 [1024, 3, 128], P(('slab', 'group')), may hold values from -6 to 6
- block_fixed: int32 [1024, 128], P(('slab', 'group')), may hold values 0 or 1
Outputs:
- disp_final: float32 [3, 262144], P(None, 'slab')
Inputs may be any that keep to these rules, and one draw needn't show every extreme that they name: `cell_nodes`: support node numbers run over the slab below, the cell's own slab and the slab above; those outside the head read zero. `block_owner`: among the 32 blocks of one device at most 4 have one owner slab, and in every draw some device has exactly 4 with one owner.
All inputs are finite; a program needn't handle non-finite values. No bound on the sum of `block_fixed` on one device may be relied on, other than what follows from the above.
Results may differ from a plain program's by a relative error of at most 0.0059.
Values may be sent and summed in bfloat16 or wider, within the bound.
No kernel may reach another device: no remote copies, remote signals or barrier semaphores. Data moves between devices by JAX's collectives and lax.ppermute only.
A program may use at most 192 MiB of HBM per device.

v0:
```python
import jax
import jax.numpy as jnp
from jax import lax
from jax.sharding import PartitionSpec as P

CAP = 4


def extended(block, sides, width):
    for axis, dim in sides:
        count = lax.axis_size(axis)
        forward = [(i, i + 1) for i in range(count - 1)]
        backward = [(target, source) for source, target in forward]
        low = lax.ppermute(
            lax.slice_in_dim(block, block.shape[dim] - width, None, axis=dim), axis, forward
        )
        high = lax.ppermute(lax.slice_in_dim(block, 0, width, axis=dim), axis, backward)
        block = jnp.concatenate([low, block, high], axis=dim)
    return block


def from_behind(array, axis, by):
    size = lax.axis_size(axis)
    pairs = [(i, i + by) for i in range(size) if 0 <= i + by < size]
    return lax.ppermute(array, axis, pairs)


def stress_of(grad, shear, bulk):
    identity = jnp.eye(3, dtype=grad.dtype)
    full = grad + identity[None, :, :, None]
    entries = [[full[:, leading, trailing] for trailing in range(3)] for leading in range(3)]
    cofactor = [
        [
            entries[(leading + 1) % 3][(trailing + 1) % 3]
            * entries[(leading + 2) % 3][(trailing + 2) % 3]
            - entries[(leading + 1) % 3][(trailing + 2) % 3]
            * entries[(leading + 2) % 3][(trailing + 1) % 3]
            for trailing in range(3)
        ]
        for leading in range(3)
    ]
    volume = (
        entries[0][0] * cofactor[0][0]
        + entries[0][1] * cofactor[0][1]
        + entries[0][2] * cofactor[0][2]
    )
    clamped = jnp.maximum(volume, 0.3)
    shear_now = shear[:, None]
    factor = (bulk[:, None] * jnp.log(clamped) - shear_now) / clamped
    rows_out = [
        jnp.stack(
            [
                shear_now * entries[leading][trailing] + factor * cofactor[leading][trailing]
                for trailing in range(3)
            ],
            axis=1,
        )
        for leading in range(3)
    ]
    return jnp.stack(rows_out, axis=1)


def body(
    disp_now,
    disp_prev,
    inv_mass,
    cell_nodes,
    shape_grads,
    cell_weights,
    cell_shear,
    cell_bulk,
    block_owner,
    block_nodes,
    block_phi,
    block_corr,
    block_target,
    block_fixed,
):
    width = disp_now.shape[1]
    slabs = lax.axis_size("slab")
    nearby = extended(disp_now.astype(jnp.bfloat16), (("slab", 1),), width)
    gathered = jnp.moveaxis(jnp.take(nearby, cell_nodes, axis=1), 0, 1)
    grad = jnp.einsum("cia,cjap->cijp", gathered, shape_grads, preferred_element_type=jnp.float32)
    stress = stress_of(grad, cell_shear, cell_bulk)
    weighted = (cell_weights[:, None, None, :] * stress).astype(jnp.bfloat16)
    force = jnp.einsum("cijp,cjap->cia", weighted, shape_grads, preferred_element_type=jnp.float32)
    partial_value = (
        jnp.zeros((3, 3 * width), jnp.float32).at[:, cell_nodes].add(jnp.moveaxis(force, 1, 0))
    )
    summed = lax.psum(partial_value, "group")
    from_above = from_behind(summed[:, :width], "slab", -1)
    from_below = from_behind(summed[:, 2 * width :], "slab", 1)
    force_sum = summed[:, width : 2 * width] + from_above + from_below
    disp_next = 2.0 * disp_now - disp_prev - inv_mass[None, :] * force_sum
    support = block_nodes.shape[1]
    owner = block_owner[:, 0]
    matches = (owner[:, None] == jnp.arange(slabs, dtype=jnp.int32)[None, :]).astype(jnp.int32)
    ranked = jnp.sum((jnp.cumsum(matches, axis=0) - matches) * matches, axis=1)
    slot_of = owner * CAP + ranked
    fixed_mask = block_fixed.astype(jnp.float32)
    highest = lax.Precision.HIGHEST
    request = jnp.zeros((slabs * CAP, support), jnp.int32).at[slot_of].set(block_nodes)
    request = request.reshape(slabs, CAP, support)
    asked = lax.all_to_all(request, "slab", split_axis=0, concat_axis=0, tiled=True)
    looked = jnp.moveaxis(jnp.take(disp_next, asked, axis=1), 0, 2)
    returned = lax.all_to_all(looked, "slab", split_axis=0, concat_axis=0, tiled=True)
    returned, asked = (returned, asked)
    values = returned.reshape(slabs * CAP, 3, support)[slot_of]
    interp = jnp.einsum("bma,bia->bim", block_phi, values, precision=highest)
    resid = fixed_mask[:, None, :] * (block_target - interp)
    corr = jnp.einsum("bmq,biq->bim", block_corr, resid, precision=highest)
    delta = jnp.einsum("bma,bim->bia", block_phi, corr, precision=highest)
    outgoing = jnp.zeros((slabs * CAP, 3, support), jnp.float32).at[slot_of].set(delta)
    arrived = lax.all_to_all(
        outgoing.reshape(slabs, CAP, 3, support), "slab", split_axis=0, concat_axis=0, tiled=True
    )
    added = jnp.zeros((3, width), jnp.float32).at[:, asked].add(jnp.moveaxis(arrived, 2, 0))
    return disp_next + lax.psum(added, "group")


def solution(mesh):
    placed = (
        P(None, "slab"),
        P(None, "slab"),
        P("slab"),
        P(("slab", "group"), None),
        P(("slab", "group"), None, None, None),
        P(("slab", "group"), None),
        P(("slab", "group")),
        P(("slab", "group")),
        P(("slab", "group"), None),
        P(("slab", "group"), None),
        P(("slab", "group"), None, None),
        P(("slab", "group"), None, None),
        P(("slab", "group"), None, None),
        P(("slab", "group"), None),
    )
    return jax.shard_map(
        body, mesh=mesh, in_specs=placed, out_specs=P(None, "slab"), check_vma=False
    )
```

profile of v0, /device:TPU:0, one launch (start us, length us, event | category | flops | bytes accessed | tf_op | source)
XLA Modules:
  0.0 435.3 jit_solution(6011149501604761152)
XLA Ops:
  6.5 1.3 convert_element_type.19
  7.8 2.4 collective-permute-start
  10.2 1.3 collective-permute-start.1
  11.6 0.8 compare_select_fusion.1
  12.3 0.1 reshape.1417
  12.4 0.8 compare_and_fusion.1
  13.2 2.7 collective-permute-done.1
  15.9 1.3 pad_maximum_fusion
  17.2 15.8 %copy.131 = bf16[3,98304]{0,1:T(8,128)(2,1)} copy(bf16[3,98304]{1,0:T(4,128)(2,1)S(1)} %pad_maximum_fusion) | data formatting | bytes 1179648 | tf_op jit(solution)/shard_map/concatenate | solution.py:18
  33.0 32.5 %gather_fusion = bf16[6144,3]{1,0:T(8,128)(2,1)} fusion(bf16[3,98304]{0,1:T(8,128)(2,1)} %copy.131, s32[6144]{0:T(1024)S(1)} %broadcast_clamp_fusion.1), kind=kCustom, calls=%fused_computation | custom fusion | bytes 98304 | tf_op jit(solution)/shard_map/jit(_take)/gather | solution.py:82
  65.5 1.9 copy.132
  67.5 3.3 fusion.10
  70.7 0.1 copy_add_fusion
  70.8 0.1 multiply_add_fusion.8
  70.9 0.1 multiply_add_fusion.7
  71.0 0.1 multiply_add_fusion.6
  71.1 4.1 convolution_bitcast_fusion
  75.2 2.2 copy.149
  77.4 53.3 %scatter_custom_fusion = f32[3,98304]{0,1:T(8,128)} fusion(s32[6144]{0:T(1024)S(1)} %reshape.1417, f32[6144,3]{1,0:T(8,128)} %bitcast.170, f32[]{:T(128)} %constant.16.clone.1), kind=kCustom, calls=%fused_computation.7 | custom fusion | flops 18432 | bytes 1180160 | tf_op jit(solution)/shard_map/scatter-add | solution.py:88
  130.7 26.7 %copy.137 = f32[3,98304]{1,0:T(4,128)} copy(f32[3,98304]{0,1:T(8,128)} %scatter_custom_fusion) | data formatting | bytes 2359296 | tf_op jit(solution)/shard_map/scatter-add | solution.py:88
  157.5 0.2 select_reduce_fusion
  157.7 0.9 scatter_custom_fusion.1
  158.7 0.6 reshape.1388
  159.3 8.0 %all-to-all-start = ((s32[8,4,256]{2,1,0:T(4,128)}), s32[8,4,256]{2,1,0:T(4,128)S(1)}, u32[]{:S(2)}, u32[]{:S(2)}) async-start(s32[8,4,256]{2,1,0:T(4,128)} %reshape.1388), calls=%async_computation | async-start | bytes 65536 | tf_op jit(solution)/shard_map/all_to_all | solution.py:104
  167.3 4.8 %all-to-all-done = s32[8,4,256]{2,1,0:T(4,128)S(1)} async-done(((s32[8,4,256]{2,1,0:T(4,128)}), s32[8,4,256]{2,1,0:T(4,128)S(1)}, u32[]{:S(2)}, u32[]{:S(2)}) %all-to-all-start) | async-done | bytes 32800 | tf_op jit(solution)/shard_map/all_to_all | solution.py:104
  172.2 59.9 %all-reduce.3.cloned.1.call-done = f32[3,98304]{1,0:T(4,128)} async-done(((f32[3,98304]{1,0:T(4,128)}), f32[3,98304]{1,0:T(4,128)}) %all-reduce.3.cloned.1.call-update) | async-done | bytes 1179664 | tf_op jit(solution)/shard_map/psum | solution.py:90
  232.1 1.4 fusion.22
  233.5 1.3 collective-permute-start.2
  234.8 3.1 collective-permute-start.3
  237.9 1.4 collective-permute-done.3
  239.4 1.6 fusion.7
  240.9 8.6 %copy.138 = f32[3,32768]{0,1:T(8,128)} copy(f32[3,32768]{1,0:T(4,128)S(1)} %fusion.7) | data formatting | bytes 786432 | tf_op jit(solution)/shard_map/sub | solution.py:94
  249.5 33.5 %gather_fusion.1 = f32[8192,3]{1,0:T(8,128)} fusion(f32[3,32768]{0,1:T(8,128)} %copy.138, s32[8192]{0:T(1024)S(1)} %broadcast_clamp_fusion), kind=kCustom, calls=%fused_computation.1 | custom fusion | bytes 229376 | tf_op jit(solution)/shard_map/jit(_take)/gather | solution.py:105
  283.0 2.8 copy.139
  285.8 0.7 select_bitcast_fusion
  286.5 13.2 %all-to-all-start.1 = ((f32[8,4,3,256]{3,1,2,0:T(4,128)}), f32[8,4,3,256]{3,1,2,0:T(4,128)S(1)}, u32[]{:S(2)}, u32[]{:S(2)}) async-start(f32[8,4,3,256]{3,1,2,0:T(4,128)} %select_bitcast_fusion), calls=%async_computation.1 | async-start | bytes 196608 | tf_op jit(solution)/shard_map/all_to_all | solution.py:106
  299.7 5.1 %all-to-all-done.1 = f32[8,4,3,256]{3,1,2,0:T(4,128)S(1)} async-done(((f32[8,4,3,256]{3,1,2,0:T(4,128)}), f32[8,4,3,256]{3,1,2,0:T(4,128)S(1)}, u32[]{:S(2)}, u32[]{:S(2)}) %all-to-all-start.1) | async-done | bytes 98336 | tf_op jit(solution)/shard_map/all_to_all | solution.py:106
  304.9 0.6 gather_fusion.2
  305.5 5.8 %fusion.4 = f32[32,3,128]{2,1,0:T(4,128)S(1)} fusion(f32[32,3,256]{2,1,0:T(4,128)S(1)} %gather_fusion.2, f32[32,128,256]{2,1,0:T(8,128)} %param.24, f32[32,3,128]{2,0,1:T(8,128)S(1)} %copy-done.4, f32[32,128]{1,0:T(8,128)S(1)} %convert_element_type.23), kind=kOutput, calls=%fused_computation.13 | convolution fusion | flops 37773312 | bytes 4407296 | tf_op jit(solution)/shard_map/bma,bia->bim/dot_general | solution.py:109
  311.4 3.4 fusion.23
  314.7 2.1 fusion.24
  316.9 1.5 scatter_fusion
  318.4 7.6 %all_to_all.15 = f32[8,4,3,256]{3,1,2,0:T(4,128)S(1)} all-to-all(f32[8,4,3,256]{3,1,2,0:T(4,128)S(1)} %copy.143), channel_id=1, replica_groups=mesh['slab'=8,'group'=4] {'slab'}, dimensions={0} | all-to-all | bytes 196608 | tf_op jit(solution)/shard_map/all_to_all | solution.py:114
  326.0 2.6 copy.151
  328.6 51.1 %scatter_custom_fusion.3 = f32[3,32768]{0,1:T(8,128)} fusion(s32[8192]{0:T(1024)S(1)} %bitcast.176, f32[8192,3]{1,0:T(8,128)} %bitcast.169, f32[]{:T(128)} %constant.16.clone.1), kind=kCustom, calls=%fused_computation.9 | custom fusion | flops 24576 | bytes 393728 | tf_op jit(solution)/shard_map/scatter-add | solution.py:117
  379.7 9.8 %copy.146 = f32[3,32768]{1,0:T(4,128)} copy(f32[3,32768]{0,1:T(8,128)} %scatter_custom_fusion.3) | data formatting | bytes 786432 | tf_op jit(solution)/shard_map/scatter-add | solution.py:117
  389.5 37.0 %all-reduce.5.cloned.1.call-done = f32[3,32768]{1,0:T(4,128)} async-done(((f32[3,32768]{1,0:T(4,128)}), f32[3,32768]{1,0:T(4,128)}) %all-reduce.5.cloned.1.call-update) | async-done | bytes 393232 | tf_op jit(solution)/shard_map/psum | solution.py:118
  426.5 2.0 add.250
  (43 shorter events, 0.5 us)
Async XLA Ops:
  6.5 304.8 %copy-start = (f32[32,128,128]{2,1,0:T(8,128)S(1)}, f32[32,128,128]{2,1,0:T(8,128)}, u32[]{:S(2)}) copy-start(f32[32,128,128]{2,1,0:T(8,128)} %param.25) | copy-start | bytes 6291460
  6.5 225.6 %all-reduce.3.cloned.1.call-start = ((), (), s32[]{:S(2)}) async-start(), calls=%async_computation.3 | async-start | bytes 3145728 | tf_op jit(solution)/shard_map/psum | solution.py:90
  7.8 5.4 %collective-permute-start = (bf16[3,32768]{1,0:T(4,128)(2,1)S(1)}, bf16[3,32768]{1,0:T(4,128)(2,1)S(1)}, u32[]{:S(2)}, u32[]{:S(2)}) collective-permute-start(bf16[3,32768]{1,0:T(4,128)(2,1)S(1)} %convert_element_type.19), channel_id=1, source_target_pairs={{0,4},{4,8},{8,12},{12,16},{16,20},{20,24},{24,28},{1,5},{5,9},{9,... | collective-permute-start | bytes 589832 | tf_op jit(solution)/shard_map/ppermute | solution.py:14
  10.2 5.6 %collective-permute-start.1 = (bf16[3,32768]{1,0:T(4,128)(2,1)S(1)}, bf16[3,32768]{1,0:T(4,128)(2,1)}, u32[]{:S(2)}, u32[]{:S(2)}) collective-permute-start(bf16[3,32768]{1,0:T(4,128)(2,1)S(1)} %convert_element_type.19), channel_id=1, source_target_pairs={{4,0},{8,4},{12,8},{16,12},{20,16},{24,20},{28,24},{5,1},{9,5},{13... | collective-permute-start | bytes 589832 | tf_op jit(solution)/shard_map/ppermute | solution.py:17
  33.0 37.8 %copy-start.7 = (f32[32]{0:T(128)S(1)}, f32[32]{0:T(128)}, u32[]{:S(2)}) copy-start(f32[32]{0:T(128)} %param.20) | copy-start | bytes 388
  33.0 37.8 %copy-start.9 = (f32[32]{0:T(128)S(1)}, f32[32]{0:T(128)}, u32[]{:S(2)}) copy-start(f32[32]{0:T(128)} %param.21) | copy-start | bytes 388
  33.0 38.1 %copy-start.6 = (f32[32,128]{1,0:T(8,128)S(1)}, f32[32,128]{1,0:T(8,128)}, u32[]{:S(2)}) copy-start(f32[32,128]{1,0:T(8,128)} %param.19) | copy-start | bytes 49156
  130.7 26.7 %copy-start.8 = (s32[32,1]{0,1:T(1,128)S(1)}, s32[32,1]{0,1:T(1,128)}, u32[]{:S(2)}) copy-start(s32[32,1]{0,1:T(1,128)} %param.22) | copy-start | bytes 388
  130.7 36.6 %copy-start.5 = (s32[32,128]{1,0:T(8,128)S(1)}, s32[32,128]{1,0:T(8,128)}, u32[]{:S(2)}) copy-start(s32[32,128]{1,0:T(8,128)} %param.27) | copy-start | bytes 49156
  157.4 82.0 %copy-start.2 = (f32[3,32768]{1,0:T(4,128)S(1)}, f32[3,32768]{1,0:T(4,128)}, u32[]{:S(2)}) copy-start(f32[3,32768]{1,0:T(4,128)} %param.14) | copy-start | bytes 1179652
  157.4 82.0 %copy-start.3 = (f32[32768]{0:T(1024)S(1)}, f32[32768]{0:T(1024)}, u32[]{:S(2)}) copy-start(f32[32768]{0:T(1024)} %param.16) | copy-start | bytes 393220
  159.3 12.8 %all-to-all-start = ((s32[8,4,256]{2,1,0:T(4,128)}), s32[8,4,256]{2,1,0:T(4,128)S(1)}, u32[]{:S(2)}, u32[]{:S(2)}) async-start(s32[8,4,256]{2,1,0:T(4,128)} %reshape.1388), calls=%async_computation | async-start | bytes 65536 | tf_op jit(solution)/shard_map/all_to_all | solution.py:104
  233.5 4.4 %collective-permute-start.2 = (f32[3,32768]{1,0:T(4,128)S(1)}, f32[3,32768]{1,0:T(4,128)S(1)}, u32[]{:S(2)}, u32[]{:S(2)}) collective-permute-start(f32[3,32768]{1,0:T(4,128)S(1)} %get-tuple-element.9), channel_id=1, source_target_pairs={{4,0},{8,4},{12,8},{16,12},{20,16},{24,20},{28,24},{5,1},{9,5},{13... | collective-permute-start | bytes 1179656 | tf_op jit(solution)/shard_map/ppermute | solution.py:25
  234.8 4.6 %collective-permute-start.3 = (f32[3,32768]{1,0:T(4,128)S(1)}, f32[3,32768]{1,0:T(4,128)S(1)}, u32[]{:S(2)}, u32[]{:S(2)}) collective-permute-start(f32[3,32768]{1,0:T(4,128)S(1)} %get-tuple-element.10), channel_id=1, source_target_pairs={{0,4},{4,8},{8,12},{12,16},{16,20},{20,24},{24,28},{1,5},{5,9},{9,... | collective-permute-start | bytes 1179656 | tf_op jit(solution)/shard_map/ppermute | solution.py:25
  249.5 56.0 %copy-start.4 = (f32[32,3,128]{2,0,1:T(8,128)S(1)}, f32[32,3,128]{2,0,1:T(8,128)}, u32[]{:S(2)}) copy-start(f32[32,3,128]{2,0,1:T(8,128)} %param.26) | copy-start | bytes 147460
  286.5 18.4 %all-to-all-start.1 = ((f32[8,4,3,256]{3,1,2,0:T(4,128)}), f32[8,4,3,256]{3,1,2,0:T(4,128)S(1)}, u32[]{:S(2)}, u32[]{:S(2)}) async-start(f32[8,4,3,256]{3,1,2,0:T(4,128)} %select_bitcast_fusion), calls=%async_computation.1 | async-start | bytes 196608 | tf_op jit(solution)/shard_map/all_to_all | solution.py:106
  299.6 126.9 %all-reduce.5.cloned.1.call-start = ((), (), s32[]{:S(2)}) async-start(), calls=%async_computation.4 | async-start | bytes 1048576 | tf_op jit(solution)/shard_map/psum | solution.py:118
  305.5 9.2 %copy-start.1 = (f32[32,128,256]{2,1,0:T(8,128)S(1)}, f32[32,128,256]{2,1,0:T(8,128)}, u32[]{:S(2)}) copy-start(f32[32,128,256]{2,1,0:T(8,128)} %param.24) | copy-start | bytes 12582916
Sparse Core Ops, SparseCore 0:
  157.5 74.5 all-reduce.2
  389.6 36.8 all-reduce.4
where the time goes:
time: 437 us; the launch traced here: 435 us
  local copies, waits for them, and re-layouts  142 us (32%)
  other arithmetic  113 us (26%)
  waiting for transfers between devices  111 us (25%)
  starting transfers between devices  29.3 us (7%)
  matrix products  18.6 us (4%)
  between operations  13.7 us (3%)
  blocking collectives  7.58 us (2%)
    psum x1, waiting for transfers between devices, body(): summed = lax.psum(partial_value, 'group')  59.9 us
    scatter-add x1, other arithmetic, body(): jnp.zeros((3, 3 * width), jnp.float32).at[:, cell_nodes]  53.3 us
    scatter-add x1, other arithmetic, body(): jnp.zeros((3, width), jnp.float32).at[:, asked]  51.1 us
    psum x1, waiting for transfers between devices, body(): return disp_next + lax.psum(added, 'group')  37 us
    gather x2, local copies, waits for them, and re-layouts, body(): looked = jnp.moveaxis(jnp.take(disp_next, asked, axis=1), 0, 2)  36.3 us
    gather x2, local copies, waits for them, and re-layouts, body(): gathered = jnp.moveaxis(jnp.take(nearby, cell_nodes, axis=1), 0, 1)  34.5 us
    scatter-add x1, local copies, waits for them, and re-layouts, body(): jnp.zeros((3, 3 * width), jnp.float32).at[:, cell_nodes]  26.7 us
    concatenate x1, local copies, waits for them, and re-layouts, extended(): block = jnp.concatenate([low, block, high], axis=dim)  15.8 us
  transfers between devices with their start and end apart: 8, of which 6 were waited for; matrix products, arithmetic and copies ran while one was open for 1% of the time, Pallas kernels for 0%

commit v1 on v0

v1 whole, which is shorter than its diff:
```python
import functools

import jax
import jax.numpy as jnp
from jax import lax
from jax.experimental import pallas as pl
from jax.experimental.pallas import tpu as pltpu
from jax.sharding import PartitionSpec as P

CAP = 4
LANES = 128
GROUP_CELLS = 8
BF = jnp.bfloat16
F32 = jnp.float32
VMEM = pl.BlockSpec(memory_space=pltpu.VMEM)
SMEM = pl.BlockSpec(memory_space=pltpu.SMEM)
PARAMS = pltpu.CompilerParams(vmem_limit_bytes=56 * 1024 * 1024)
NT = (((1,), (1,)), ((), ()))
NN = (((1,), (0,)), ((), ()))


def call(kernel, outs, in_specs, out_specs=None, **extra):
    return pl.pallas_call(
        kernel,
        out_shape=outs,
        in_specs=in_specs,
        out_specs=jax.tree.map(lambda _: VMEM, outs) if out_specs is None else out_specs,
        compiler_params=PARAMS,
        **extra,
    )


def shape_of(dims, dtype):
    return jax.ShapeDtypeStruct(dims, dtype)


def dot(left, right, dims=NN):
    return lax.dot_general(left, right, dims, preferred_element_type=F32)


def one_hot(rows, line):
    places = lax.broadcasted_iota(jnp.int32, (rows, line.shape[1]), 0)
    return jnp.where(places == line, 1.0, 0.0).astype(BF)


def table_kernel(now_ref, out_ref):
    for part in range(3):
        out_ref[pl.ds(part * LANES, LANES), :] = now_ref[part].T.astype(BF)


def request_kernel(slabs, owner_ref, nodes_ref, request_ref, slot_ref):
    request_ref[...] = jnp.zeros_like(request_ref)

    def step(block, counts):
        owner = owner_ref[block]
        rank = jnp.int32(0)
        for slab in range(slabs):
            rank = jnp.where(owner == slab, counts[slab], rank)
        slot = owner * CAP + rank
        slot_ref[block] = slot
        request_ref[pl.ds(slot, 1), :] = nodes_ref[pl.ds(block, 1), :]
        return tuple(counts[slab] + (owner == slab).astype(jnp.int32) for slab in range(slabs))

    lax.fori_loop(0, nodes_ref.shape[0], step, (jnp.int32(0),) * slabs)


def stress_of(full, shear, bulk):
    cofactor = [
        [
            full[(a + 1) % 3][(b + 1) % 3] * full[(a + 2) % 3][(b + 2) % 3]
            - full[(a + 1) % 3][(b + 2) % 3] * full[(a + 2) % 3][(b + 1) % 3]
            for b in range(3)
        ]
        for a in range(3)
    ]
    volume = (
        full[0][0] * cofactor[0][0] + full[0][1] * cofactor[0][1] + full[0][2] * cofactor[0][2]
    )
    clamped = jnp.maximum(volume, 0.3)
    factor = (bulk * jnp.log(clamped) - shear) / clamped
    return [[shear * full[a][b] + factor * cofactor[a][b] for b in range(3)] for a in range(3)]


def cell_kernel(
    low_ref, own_ref, high_ref, nodes_ref, grads_ref, weights_ref, shear_ref, bulk_ref,
    out_ref, total_ref,
):
    step = pl.program_id(0)

    @pl.when(step == 0)
    def _():
        total_ref[...] = jnp.zeros_like(total_ref)

    nodes = nodes_ref[0]
    count = nodes.shape[1]
    cells, _, support, points = grads_ref.shape
    rows = own_ref.shape[1]
    hot = one_hot(3 * rows, nodes >> 7)
    table = jnp.concatenate([low_ref[...], own_ref[...], high_ref[...]], axis=1)
    picked = dot(table, hot)
    low_place = lax.broadcasted_iota(jnp.int32, (LANES, count), 0)
    mask = low_place == (nodes & (LANES - 1))
    cell_mask = (
        lax.broadcasted_iota(jnp.int32, (cells, count), 1) // support
        == lax.broadcasted_iota(jnp.int32, (cells, count), 0)
    )
    left = jnp.concatenate(
        [
            jnp.where(
                cell_mask,
                jnp.sum(
                    jnp.where(mask, picked[part * LANES : (part + 1) * LANES], 0.0),
                    axis=0,
                    keepdims=True,
                ),
                0.0,
            )
            for part in range(3)
        ],
        axis=0,
    ).astype(BF)
    slopes = [grads_ref[:, axis].reshape(count, points) for axis in range(3)]
    grad = [dot(left, slopes[axis]) for axis in range(3)]
    full = [
        [
            grad[b][a * cells : (a + 1) * cells] + (1.0 if a == b else 0.0)
            for b in range(3)
        ]
        for a in range(3)
    ]
    stress = stress_of(full, shear_ref[...], bulk_ref[...])
    weights = weights_ref[...]
    back = None
    for axis in range(3):
        wide = jnp.concatenate([weights * stress[a][axis] for a in range(3)], axis=0).astype(BF)
        term = dot(wide, slopes[axis], NT)
        back = term if back is None else back + term
    scattered = []
    for part in range(3):
        line = jnp.sum(
            jnp.where(cell_mask, back[part * cells : (part + 1) * cells], 0.0),
            axis=0,
            keepdims=True,
        )
        scattered.append(jnp.where(mask, line, 0.0).astype(BF))
    total_ref[...] += dot(jnp.concatenate(scattered, axis=0), hot, NT)

    @pl.when(step == pl.num_programs(0) - 1)
    def _():
        for part in range(3):
            plane = total_ref[pl.ds(part * LANES, LANES), :]
            for slab in range(3):
                out_ref[slab, part] = plane[:, slab * rows : (slab + 1) * rows].T.astype(BF)


def combine_kernel(quarters, place_ref, own_ref, up_ref, down_ref, *outs):
    depth = own_ref.shape[1] // quarters
    for shift in range(quarters):
        first = lax.rem(place_ref[0] + shift, quarters) * depth
        window = pl.ds(pl.multiple_of(first, depth), depth)
        for part in range(3):
            outs[shift][part] = (
                own_ref[part, window, :].astype(F32)
                + up_ref[part, window, :].astype(F32)
                + down_ref[part, window, :].astype(F32)
            ).astype(BF)


def advance_kernel(
    quarters, place_ref, now_ref, prev_ref, mass_ref, *refs
):
    parts, next_ref, send_ref = refs[:quarters], refs[quarters], refs[quarters + 1]
    depth = next_ref.shape[1]
    window = pl.ds(pl.multiple_of(place_ref[0] * depth, depth), depth)
    mass = mass_ref[window, :]
    for part in range(3):
        force = parts[0][part].astype(F32)
        for other in parts[1:]:
            force = force + other[part].astype(F32)
        value = 2.0 * now_ref[part, window, :] - prev_ref[part, window, :] - mass * force
        next_ref[part] = value
        send_ref[part] = value.astype(BF)


def lookup_kernel(quarters, slabs, place_ref, asked_ref, *refs):
    parts, out_ref, table_ref = refs[:quarters], refs[quarters], refs[quarters + 1]
    depth = parts[0].shape[1]
    gathered = refs[quarters + 2]
    for shift in range(quarters):
        owner = lax.rem(place_ref[0] - shift + quarters, quarters)
        window = pl.ds(pl.multiple_of(owner * depth, depth), depth)
        for part in range(3):
            gathered[part, window, :] = parts[shift][part].astype(F32)
    rows = depth * quarters
    for part in range(3):
        table_ref[pl.ds(part * LANES, LANES), :] = gathered[part].T.astype(BF)
    support = asked_ref.shape[2]
    pad = jnp.zeros((out_ref.shape[1] - 3 * CAP, support), F32)

    def step(slab, carry):
        lines = asked_ref[slab]
        low_place = lax.broadcasted_iota(jnp.int32, (LANES, support), 0)
        found = [[], [], []]
        for slot in range(CAP):
            line = lines[slot : slot + 1]
            picked = dot(table_ref[...], one_hot(rows, line >> 7))
            mask = low_place == (line & (LANES - 1))
            for part in range(3):
                found[part].append(
                    jnp.sum(
                        jnp.where(mask, picked[part * LANES : (part + 1) * LANES], 0.0),
                        axis=0,
                        keepdims=True,
                    )
                )
        out_ref[slab] = jnp.concatenate(found[0] + found[1] + found[2] + [pad], axis=0).astype(BF)
        return carry

    lax.fori_loop(0, slabs, step, 0)


def block_kernel(slot_ref, values_ref, phi_ref, corr_ref, target_ref, fixed_ref, out_ref, hold, sent):
    step = pl.program_id(0)
    slabs, height, support = values_ref.shape
    blocks = phi_ref.shape[0]

    @pl.when(step == 0)
    def _():
        for slab in range(slabs):
            hold[slab] = values_ref[slab].astype(F32)
        sent[...] = jnp.zeros_like(sent)

    pad = jnp.zeros((5, support), F32)
    for local in range(blocks):
        slot = slot_ref[step * blocks + local]
        slab, rank = slot // CAP, lax.rem(slot, CAP)
        value = jnp.concatenate(
            [hold[slab, pl.ds(part * CAP + rank, 1), :] for part in range(3)] + [pad], axis=0
        ).astype(BF)
        phi = phi_ref[local].astype(BF)
        interp = dot(value, phi, NT)
        goal = jnp.concatenate([target_ref[local], jnp.zeros((5, phi.shape[0]), F32)], axis=0)
        resid = fixed_ref[local : local + 1].astype(F32) * (goal - interp)
        corr = dot(resid.astype(BF), corr_ref[local].astype(BF), NT)
        delta = dot(corr.astype(BF), phi)
        for part in range(3):
            sent[slab, pl.ds(part * CAP + rank, 1), :] = delta[part : part + 1]

    @pl.when(step == pl.num_programs(0) - 1)
    def _():
        for slab in range(slabs):
            out_ref[slab] = sent[slab].astype(BF)


def spread_kernel(quarters, slabs, place_ref, asked_ref, arrived_ref, *refs):
    outs, total_ref = refs[:quarters], refs[quarters]
    depth = outs[0].shape[1]
    rows = depth * quarters
    support = asked_ref.shape[2]
    total_ref[...] = jnp.zeros_like(total_ref)

    def step(slab, carry):
        lines = asked_ref[slab]
        values = arrived_ref[slab].astype(F32)
        low_place = lax.broadcasted_iota(jnp.int32, (LANES, support), 0)
        wide, hots = [], []
        for slot in range(CAP):
            line = lines[slot : slot + 1]
            mask = low_place == (line & (LANES - 1))
            wide.append(
                jnp.concatenate(
                    [
                        jnp.where(mask, values[part * CAP + slot : part * CAP + slot + 1], 0.0)
                        for part in range(3)
                    ],
                    axis=0,
                ).astype(BF)
            )
            hots.append(one_hot(rows, line >> 7))
        total_ref[...] += dot(jnp.concatenate(wide, axis=1), jnp.concatenate(hots, axis=1), NT)
        return carry

    lax.fori_loop(0, slabs, step, 0)
    natural = refs[quarters + 1]
    for part in range(3):
        natural[part] = total_ref[pl.ds(part * LANES, LANES), :].T
    for shift in range(quarters):
        first = lax.rem(place_ref[0] + shift, quarters) * depth
        window = pl.ds(pl.multiple_of(first, depth), depth)
        for part in range(3):
            outs[shift][part] = natural[part, window, :].astype(BF)


def finish_kernel(next_ref, *refs):
    out_ref = refs[-1]
    for part in range(3):
        value = refs[0][part].astype(F32)
        for other in refs[1:-1]:
            value = value + other[part].astype(F32)
        out_ref[part] = next_ref[part] + value


def gather_kernel(quarters, place_ref, *refs):
    parts, out_ref = refs[:quarters], refs[quarters]
    depth = parts[0].shape[1]
    for shift in range(quarters):
        owner = lax.rem(place_ref[0] - shift + quarters, quarters)
        window = pl.ds(pl.multiple_of(owner * depth, depth), depth)
        for part in range(3):
            out_ref[part, window, :] = parts[shift][part]


def shifted(array, axis, by, wrap):
    size = lax.axis_size(axis)
    if wrap:
        pairs = [(i, (i + by) % size) for i in range(size)]
    else:
        pairs = [(i, i + by) for i in range(size) if 0 <= i + by < size]
    return lax.ppermute(array, axis, pairs)


def body(
    disp_now,
    disp_prev,
    inv_mass,
    cell_nodes,
    shape_grads,
    cell_weights,
    cell_shear,
    cell_bulk,
    block_owner,
    block_nodes,
    block_phi,
    block_corr,
    block_target,
    block_fixed,
):
    width = disp_now.shape[1]
    slabs = lax.axis_size("slab")
    quarters = lax.axis_size("group")
    rows = width // LANES
    depth = rows // quarters
    place = lax.axis_index("group").astype(jnp.int32).reshape(1)
    now = disp_now.reshape(3, rows, LANES)
    prev = disp_prev.reshape(3, rows, LANES)
    mass = inv_mass.reshape(rows, LANES)

    own = call(table_kernel, shape_of((3 * LANES, rows), BF), [VMEM])(now)
    low = shifted(own, "slab", 1, False)
    high = shifted(own, "slab", -1, False)

    blocks, support = block_nodes.shape
    request, slot = call(
        functools.partial(request_kernel, slabs),
        (shape_of((slabs * CAP, support), jnp.int32), shape_of((blocks,), jnp.int32)),
        [SMEM, VMEM],
        (VMEM, SMEM),
    )(block_owner.reshape(blocks), block_nodes)
    asked = lax.all_to_all(
        request.reshape(slabs, CAP, support), "slab", split_axis=0, concat_axis=0, tiled=True
    )

    cells, _, count, points = shape_grads.shape
    steps = cells // GROUP_CELLS
    lines = cell_nodes.reshape(steps, 1, GROUP_CELLS * count)
    partial = pl.pallas_call(
        cell_kernel,
        out_shape=shape_of((3, 3, rows, LANES), BF),
        grid=(steps,),
        in_specs=[
            pl.BlockSpec((3 * LANES, rows), lambda s: (0, 0)),
            pl.BlockSpec((3 * LANES, rows), lambda s: (0, 0)),
            pl.BlockSpec((3 * LANES, rows), lambda s: (0, 0)),
            pl.BlockSpec((1, 1, GROUP_CELLS * count), lambda s: (s, 0, 0)),
            pl.BlockSpec((GROUP_CELLS, 3, count, points), lambda s: (s, 0, 0, 0)),
            pl.BlockSpec((GROUP_CELLS, points), lambda s: (s, 0)),
            pl.BlockSpec((GROUP_CELLS, 1), lambda s: (s, 0)),
            pl.BlockSpec((GROUP_CELLS, 1), lambda s: (s, 0)),
        ],
        out_specs=pl.BlockSpec((3, 3, rows, LANES), lambda s: (0, 0, 0, 0)),
        scratch_shapes=[pltpu.VMEM((3 * LANES, 3 * rows), F32)],
        compiler_params=PARAMS,
    )(
        low, own, high, lines, shape_grads, cell_weights,
        cell_shear.reshape(cells, 1), cell_bulk.reshape(cells, 1),
    )

    from_above = shifted(partial[0], "slab", -1, False)
    from_below = shifted(partial[2], "slab", 1, False)
    quarter = (3, depth, LANES)
    pieces = call(
        functools.partial(combine_kernel, quarters),
        (shape_of(quarter, BF),) * quarters,
        [SMEM] + [VMEM] * 3,
    )(place, partial[1], from_above, from_below)
    pieces = [pieces[0]] + [
        shifted(pieces[by], "group", by, True) for by in range(1, quarters)
    ]
    mine, sent = call(
        functools.partial(advance_kernel, quarters),
        (shape_of(quarter, F32), shape_of(quarter, BF)),
        [SMEM] + [VMEM] * (3 + quarters),
    )(place, now, prev, mass, *pieces)
    tables = [sent] + [shifted(sent, "group", by, True) for by in range(1, quarters)]
    height = -(-3 * CAP // 16) * 16
    looked = call(
        functools.partial(lookup_kernel, quarters, slabs),
        shape_of((slabs, height, support), BF),
        [SMEM] + [VMEM] * (1 + quarters),
        scratch_shapes=[
            pltpu.VMEM((3 * LANES, rows), BF),
            pltpu.VMEM((3, rows, LANES), F32),
        ],
    )(place, asked, *tables)
    values = lax.all_to_all(looked, "slab", split_axis=0, concat_axis=0, tiled=True)

    each = 8
    border = block_phi.shape[1]
    outgoing = pl.pallas_call(
        block_kernel,
        out_shape=shape_of((slabs, height, support), BF),
        grid=(blocks // each,),
        in_specs=[
            SMEM,
            pl.BlockSpec((slabs, height, support), lambda s: (0, 0, 0)),
            pl.BlockSpec((each, border, support), lambda s: (s, 0, 0)),
            pl.BlockSpec((each, border, border), lambda s: (s, 0, 0)),
            pl.BlockSpec((each, 3, border), lambda s: (s, 0, 0)),
            pl.BlockSpec((each, border), lambda s: (s, 0)),
        ],
        out_specs=pl.BlockSpec((slabs, height, support), lambda s: (0, 0, 0)),
        scratch_shapes=[
            pltpu.VMEM((slabs, height, support), F32),
            pltpu.VMEM((slabs, height, support), F32),
        ],
        compiler_params=PARAMS,
    )(slot, values, block_phi, block_corr, block_target, block_fixed)
    arrived = lax.all_to_all(outgoing, "slab", split_axis=0, concat_axis=0, tiled=True)
    added = call(
        functools.partial(spread_kernel, quarters, slabs),
        (shape_of(quarter, BF),) * quarters,
        [SMEM] + [VMEM] * 2,
        scratch_shapes=[
            pltpu.VMEM((3 * LANES, rows), F32),
            pltpu.VMEM((3, rows, LANES), F32),
        ],
    )(place, asked, arrived)
    added = [added[0]] + [shifted(added[by], "group", by, True) for by in range(1, quarters)]
    final = call(finish_kernel, shape_of(quarter, F32), [VMEM] * (1 + quarters))(mine, *added)
    finals = [final] + [shifted(final, "group", by, True) for by in range(1, quarters)]
    whole = call(
        functools.partial(gather_kernel, quarters),
        shape_of((3, rows, LANES), F32),
        [SMEM] + [VMEM] * quarters,
    )(place, *finals)
    return whole.reshape(3, width)


def solution(mesh):
    placed = (
        P(None, "slab"),
        P(None, "slab"),
        P("slab"),
        P(("slab", "group"), None),
        P(("slab", "group"), None, None, None),
        P(("slab", "group"), None),
        P(("slab", "group")),
        P(("slab", "group")),
        P(("slab", "group"), None),
        P(("slab", "group"), None),
        P(("slab", "group"), None, None),
        P(("slab", "group"), None, None),
        P(("slab", "group"), None, None),
        P(("slab", "group"), None),
    )
    return jax.shard_map(
        body, mesh=mesh, in_specs=placed, out_specs=P(None, "slab"), check_vma=False
    )
```

time: 437 us -> 140 us (0.32)
  local copies, waits for them, and re-layouts: 142 us -> 18.2 us
  other arithmetic: 113 us -> 0 us
  waiting for transfers between devices: 111 us -> 18 us
  Pallas kernels: 0 us -> 47.2 us
  matrix products: 18.6 us -> 0 us
  blocking collectives: 7.58 us -> 22.3 us
  between operations: 13.7 us -> 0.14 us
    scatter-add x2 -> x0, other arithmetic: 104 us -> none  [the longest x1 53.3 us: body(): jnp.zeros((3, 3 * width), jnp.float32).at[:, cell_nodes]]
    psum x2 -> x0, waiting for transfers between devices: 96.9 us -> none  [the longest x1 59.9 us: body(): summed = lax.psum(partial_value, 'group')]
    gather x5 -> x0, local copies, waits for them, and re-layouts: 71.4 us -> none  [the longest x2 36.3 us: body(): looked = jnp.moveaxis(jnp.take(disp_next, asked, axis=1), 0, 2)]
    pallas_call x0 -> x10, Pallas kernels: none -> 47.2 us  [the longest x1 17.8 us: body(): pl.pallas_call(cell_kernel, out_shape=shape_of((3, 3, rows, LANES), BF),...]
    scatter-add x2 -> x0, local copies, waits for them, and re-layouts: 36.5 us -> none  [the longest x1 26.7 us: body(): jnp.zeros((3, 3 * width), jnp.float32).at[:, cell_nodes]]
    ppermute x4 -> x16, starting transfers between devices: 8.06 us -> 29.4 us  [shifted(): return lax.ppermute(array, axis, pairs)]
    dot_general x5 -> x0, matrix products: 18.6 us -> none  [the longest x1 5.84 us: body(): interp = jnp.einsum('bma,bia->bim', block_phi, values, precision=highest)]
    concatenate x1 -> x0, local copies, waits for them, and re-layouts: 15.8 us -> none  [extended(): block = jnp.concatenate([low, block, high], axis=dim)]
  transfers between devices with their start and end apart: 8 -> 17, of which waited for: 6 -> 9; matrix products, arithmetic and copies ran while one was open for 1% -> 5% of each run, Pallas kernels for 0% -> 2%
where the time goes in v1:
time: 140 us; the launch traced here: 139 us
  Pallas kernels  47.2 us (34%)
  starting transfers between devices  32.7 us (23%)
  blocking collectives  22.3 us (16%)
  local copies, waits for them, and re-layouts  18.2 us (13%)
  waiting for transfers between devices  18 us (13%)
    ppermute x16, starting transfers between devices, shifted(): return lax.ppermute(array, axis, pairs)  29.4 us
    pallas_call x1, Pallas kernels, body(): pl.pallas_call(cell_kernel, out_shape=shape_of((3, 3, rows, LANES), BF),...  17.8 us
    ppermute x16, waiting for transfers between devices, shifted(): return lax.ppermute(array, axis, pairs)  13.7 us
    all_to_all x1, blocking collectives, body(): lax.all_to_all(request.reshape(slabs, CAP, support), 'slab', split_axis=0...  13.4 us
    unnamed x42, local copies, waits for them, and re-layouts  11.5 us
    all_to_all x1, blocking collectives, body(): lax.all_to_all(outgoing, 'slab', split_axis=0, concat_axis=0, tiled=True)  8.97 us
    pallas_call x1, Pallas kernels, body(): pl.pallas_call(block_kernel, out_shape=shape_of((slabs, height, support),...  8.26 us
    pallas_call x1, Pallas kernels, body(): call(functools.partial(spread_kernel, quarters, slabs), (shape_of(quarter...  5.05 us
  transfers between devices with their start and end apart: 17, of which 9 were waited for; matrix products, arithmetic and copies ran while one was open for 5% of the time, Pallas kernels for 2%

profile of v1, /device:TPU:0, one launch (start us, length us, event | category | flops | bytes accessed | tf_op | source)
XLA Modules:
  0.0 138.6 jit_solution(3265805807297595340)
XLA Ops:
  0.0 1.8 %copy.26 = f32[1,3,256,128]{3,2,1,0:T(8,128)} copy(f32[1,3,256,128]{3,1,2,0:T(4,128)} %bitcast.27) | data formatting | bytes 786432
  1.8 1.9 %shard_map.136.own_ref = bf16[384,256]{1,0:T(8,128)(2,1)} custom-call(f32[3,256,128]{2,1,0:T(8,128)} %bitcast.23), custom_call_target="tpu_custom_call" | custom-call | tf_op jit(solution)/shard_map/pallas_call | solution.py:348
  3.7 2.4 %collective-permute-start = (bf16[384,256]{1,0:T(8,128)(2,1)}, bf16[384,256]{1,0:T(8,128)(2,1)S(1)}, u32[]{:S(2)}, u32[]{:S(2)}) collective-permute-start(bf16[384,256]{1,0:T(8,128)(2,1)} %shard_map.136.own_ref), channel_id=1, source_target_pairs={{0,4},{4,8},{8,12},{12,16},{16,20},{20,24},{24,28},{1,5},{5,9},{9,... | collective-permute-start | bytes 589832 | tf_op jit(solution)/shard_map/ppermute | solution.py:319
  6.1 1.3 collective-permute-start.1
  7.4 1.4 %reshape.34.nodes_ref = s32[4,1,1536]{2,1,0:T(1,128)} reshape(s32[32,192]{1,0:T(8,128)} %param.17) | data formatting | bytes 49152 | tf_op jit(solution)/shard_map/reshape | solution.py:365
  8.8 1.3 copy.15.shear_ref
  10.2 1.3 copy.16.bulk_ref
  12.2 0.7 copy-done.3
  12.9 17.8 %shard_map.137 = bf16[3,3,256,128]{3,2,1,0:T(8,128)(2,1)} custom-call(bf16[384,256]{1,0:T(8,128)(2,1)} %copy-done.2, bf16[384,256]{1,0:T(8,128)(2,1)} %shard_map.136.own_ref, bf16[384,256]{1,0:T(8,128)(2,1)} %copy-done.3, s32[4,1,1536]{2,1,0:T(1,128)} %reshape.34.nodes_ref, bf16[32,3,192,128]{3,2,1,0:T(8,128)(2,1)} %grads_ref.1, f32[32,128]{1,0:T(8,128)} %weights_ref.1, ...), custom_call_target="tpu_custom_call" | custom-call | tf_op jit(solution)/shard_map/pallas_call | solution.py:366
  30.7 1.8 %slice_bitcast_fusion = (bf16[3,256,128]{2,1,0:T(8,128)(2,1)S(1)}, bf16[3,256,128]{2,1,0:T(8,128)(2,1)S(1)}, bf16[3,256,128]{2,1,0:T(8,128)(2,1)}) fusion(bf16[3,3,256,128]{3,2,1,0:T(8,128)(2,1)} %shard_map.137), kind=kLoop, calls=%fused_computation.3 | loop fusion | bytes 1179648 | tf_op jit(solution)/shard_map/squeeze | solution.py:389
  32.5 1.3 collective-permute-start.2
  33.8 6.2 %collective-permute-start.3 = (bf16[3,256,128]{2,1,0:T(8,128)(2,1)S(1)}, bf16[3,256,128]{2,1,0:T(8,128)(2,1)S(1)}, u32[]{:S(2)}, u32[]{:S(2)}) collective-permute-start(bf16[3,256,128]{2,1,0:T(8,128)(2,1)S(1)} %get-tuple-element.29), channel_id=1, source_target_pairs={{0,4},{4,8},{8,12},{12,16},{16,20},{20,24},{24,28},{1,5},{5,9},{9,... | collective-permute-start | bytes 589832 | tf_op jit(solution)/shard_map/ppermute | solution.py:319
  40.1 1.0 collective-permute-done.3.down_ref
  41.1 0.7 copy-done.5
  41.7 1.8 %shard_map.138 = (bf16[3,64,128]{2,1,0:T(8,128)(2,1)}, bf16[3,64,128]{2,1,0:T(8,128)(2,1)}, bf16[3,64,128]{2,1,0:T(8,128)(2,1)}, bf16[3,64,128]{2,1,0:T(8,128)(2,1)}) custom-call(s32[1]{0:T(128)} %bitcast.place_ref, bf16[3,256,128]{2,1,0:T(8,128)(2,1)} %get-tuple-element.31.own_ref, bf16[3,256,128]{2,1,0:T(8,128)(2,1)} %copy-done.4, ...), custom_call_target="tpu_custom_call" | custom-call | tf_op jit(solution)/shard_map/pallas_call | solution.py:391
  43.6 1.6 %collective-permute-start.4 = (bf16[3,64,128]{2,1,0:T(8,128)(2,1)}, bf16[3,64,128]{2,1,0:T(8,128)(2,1)S(1)}, u32[]{:S(2)}, u32[]{:S(2)}) collective-permute-start(bf16[3,64,128]{2,1,0:T(8,128)(2,1)} %get-tuple-element.18), channel_id=1, source_target_pairs={{0,1},{1,2},{2,3},{3,0},{4,5},{5,6},{6,7},{7,4},{8,9},{9,10},{10,1... | collective-permute-start | bytes 147464 | tf_op jit(solution)/shard_map/ppermute | solution.py:319
  45.2 2.6 %collective-permute-start.5 = (bf16[3,64,128]{2,1,0:T(8,128)(2,1)}, bf16[3,64,128]{2,1,0:T(8,128)(2,1)S(1)}, u32[]{:S(2)}, u32[]{:S(2)}) collective-permute-start(bf16[3,64,128]{2,1,0:T(8,128)(2,1)} %get-tuple-element.19), channel_id=1, source_target_pairs={{0,2},{1,3},{2,0},{3,1},{4,6},{5,7},{6,4},{7,5},{8,10},{9,11},{10,... | collective-permute-start | bytes 147464 | tf_op jit(solution)/shard_map/ppermute | solution.py:319
  47.7 1.4 collective-permute-start.6
  49.1 0.8 copy.25
  50.4 2.7 %collective-permute-done.6.refs_3_ = bf16[3,64,128]{2,1,0:T(8,128)(2,1)S(1)} collective-permute-done((bf16[3,64,128]{2,1,0:T(8,128)(2,1)}, bf16[3,64,128]{2,1,0:T(8,128)(2,1)S(1)}, u32[]{:S(2)}, u32[]{:S(2)}) %collective-permute-start.6) | collective-permute-done | bytes 49184 | tf_op jit(solution)/shard_map/ppermute | solution.py:319
  53.7 1.9 %shard_map.139 = (f32[3,64,128]{2,1,0:T(8,128)}, bf16[3,64,128]{2,1,0:T(8,128)(2,1)}) custom-call(s32[1]{0:T(128)} %bitcast.place_ref, f32[3,256,128]{2,1,0:T(8,128)} %bitcast.24, f32[3,256,128]{2,1,0:T(8,128)} %bitcast.25, f32[256,128]{1,0:T(8,128)} %bitcast.29, bf16[3,64,128]{2,1,0:T(8,128)(2,1)} %get-tuple-element.17.refs_0_, ...), custom_call_target="tpu_custom_call" | custom-call | tf_op jit(solution)/shard_map/pallas_call | solution.py:399
  55.7 2.6 %collective-permute-start.8 = (bf16[3,64,128]{2,1,0:T(8,128)(2,1)}, bf16[3,64,128]{2,1,0:T(8,128)(2,1)S(1)}, u32[]{:S(2)}, u32[]{:S(2)}) collective-permute-start(bf16[3,64,128]{2,1,0:T(8,128)(2,1)} %get-tuple-element.24.refs_0_), channel_id=1, source_target_pairs={{0,2},{1,3},{2,0},{3,1},{4,6},{5,7},{6,4},{7,5},{8,10},{9,11},{10,... | collective-permute-start | bytes 147464 | tf_op jit(solution)/shard_map/ppermute | solution.py:319
  58.3 1.1 collective-permute-start.9
  59.4 2.1 %shard_map.140 = (s32[32,256]{1,0:T(8,128)}, s32[32]{0:T(128)}) custom-call(s32[32]{0:T(128)} %bitcast.30, s32[32,256]{1,0:T(8,128)} %nodes_ref.1), custom_call_target="tpu_custom_call" | custom-call | tf_op jit(solution)/shard_map/pallas_call | solution.py:353
  61.5 0.8 reshape.38
  62.3 13.4 %all_to_all.15.asked_ref = s32[8,4,256]{2,1,0:T(4,128)} all-to-all(s32[8,4,256]{2,1,0:T(4,128)S(1)} %reshape.38), channel_id=1, replica_groups=mesh['slab'=8,'group'=4] {'slab'}, dimensions={0} | all-to-all | bytes 65536 | tf_op jit(solution)/shard_map/all_to_all | solution.py:359
  76.3 0.6 copy-done.17
  76.9 5.0 %shard_map.141 = bf16[8,16,256]{2,1,0:T(8,128)(2,1)} custom-call(s32[1]{0:T(128)} %bitcast.place_ref, s32[8,4,256]{2,1,0:T(4,128)} %all_to_all.15.asked_ref, bf16[3,64,128]{2,1,0:T(8,128)(2,1)} %get-tuple-element.24.refs_0_, bf16[3,64,128]{2,1,0:T(8,128)(2,1)} %copy-done.13, bf16[3,64,128]{2,1,0:T(8,128)(2,1)} %copy-done.15, bf16[3,64,128]{2,1,0:T(8,128)(2,1)} %copy-done.17), custom_call_target="tpu_custom_call" | custom-call | tf_op jit(solution)/shard_map/pallas_call | solution.py:406
  81.9 3.4 %all-to-all-start.1 = ((bf16[8,16,256]{2,1,0:T(8,128)(2,1)}), bf16[8,16,256]{2,1,0:T(8,128)(2,1)S(1)}, u32[]{:S(2)}, u32[]{:S(2)}) async-start(bf16[8,16,256]{2,1,0:T(8,128)(2,1)} %shard_map.141), calls=%async_computation.1 | async-start | bytes 131072 | tf_op jit(solution)/shard_map/all_to_all | solution.py:415
  85.3 0.7 copy.17.target_ref
  85.9 4.3 %all-to-all-done.1.values_ref = bf16[8,16,256]{2,1,0:T(8,128)(2,1)S(1)} async-done(((bf16[8,16,256]{2,1,0:T(8,128)(2,1)}), bf16[8,16,256]{2,1,0:T(8,128)(2,1)S(1)}, u32[]{:S(2)}, u32[]{:S(2)}) %all-to-all-start.1) | async-done | bytes 65568 | tf_op jit(solution)/shard_map/all_to_all | solution.py:415
  90.2 0.6 copy-done.1
  90.9 8.3 %shard_map.142 = bf16[8,16,256]{2,1,0:T(8,128)(2,1)} custom-call(s32[32]{0:T(128)} %get-tuple-element.23.slot_ref, bf16[8,16,256]{2,1,0:T(8,128)(2,1)} %copy-done.1, f32[32,128,256]{2,1,0:T(8,128)} %phi_ref.1, f32[32,128,128]{2,1,0:T(8,128)} %corr_ref.1, f32[32,3,128]{2,1,0:T(4,128)} %copy.17.target_ref, s32[32,128]{1,0:T(8,128)} %fixed_ref.1), custom_call_target="tpu_custom_call" | custom-call | tf_op jit(solution)/shard_map/pallas_call | solution.py:419
  99.1 9.0 %all_to_all.16.arrived_ref = bf16[8,16,256]{2,1,0:T(8,128)(2,1)} all-to-all(bf16[8,16,256]{2,1,0:T(8,128)(2,1)} %shard_map.142), channel_id=1, replica_groups=mesh['slab'=8,'group'=4] {'slab'}, dimensions={0} | all-to-all | bytes 131072 | tf_op jit(solution)/shard_map/all_to_all | solution.py:438
  108.1 5.0 %shard_map.143 = (bf16[3,64,128]{2,1,0:T(8,128)(2,1)}, bf16[3,64,128]{2,1,0:T(8,128)(2,1)}, bf16[3,64,128]{2,1,0:T(8,128)(2,1)}, bf16[3,64,128]{2,1,0:T(8,128)(2,1)}) custom-call(s32[1]{0:T(128)} %bitcast.place_ref, s32[8,4,256]{2,1,0:T(4,128)} %all_to_all.15.asked_ref, bf16[8,16,256]{2,1,0:T(8,128)(2,1)} %all_to_all.16.arrived_ref), custom_call_target="tpu_custom_call" | custom-call | tf_op jit(solution)/shard_map/pallas_call | solution.py:439
  113.1 1.9 %collective-permute-start.10 = (bf16[3,64,128]{2,1,0:T(8,128)(2,1)}, bf16[3,64,128]{2,1,0:T(8,128)(2,1)S(1)}, u32[]{:S(2)}, u32[]{:S(2)}) collective-permute-start(bf16[3,64,128]{2,1,0:T(8,128)(2,1)} %get-tuple-element.26), channel_id=1, source_target_pairs={{0,1},{1,2},{2,3},{3,0},{4,5},{5,6},{6,7},{7,4},{8,9},{9,10},{10,1... | collective-permute-start | bytes 147464 | tf_op jit(solution)/shard_map/ppermute | solution.py:319
  115.1 2.9 %collective-permute-start.12 = (bf16[3,64,128]{2,1,0:T(8,128)(2,1)}, bf16[3,64,128]{2,1,0:T(8,128)(2,1)S(1)}, u32[]{:S(2)}, u32[]{:S(2)}) collective-permute-start(bf16[3,64,128]{2,1,0:T(8,128)(2,1)} %get-tuple-element.28), channel_id=1, source_target_pairs={{0,3},{1,0},{2,1},{3,2},{4,7},{5,4},{6,5},{7,6},{8,11},{9,8},{10,9... | collective-permute-start | bytes 147464 | tf_op jit(solution)/shard_map/ppermute | solution.py:319
  118.1 1.3 collective-permute-done.10.refs_1_
  119.4 1.9 %collective-permute-done.11.refs_2_ = bf16[3,64,128]{2,1,0:T(8,128)(2,1)S(1)} collective-permute-done((bf16[3,64,128]{2,1,0:T(8,128)(2,1)}, bf16[3,64,128]{2,1,0:T(8,128)(2,1)S(1)}, u32[]{:S(2)}, u32[]{:S(2)}) %collective-permute-start.11) | collective-permute-done | bytes 49184 | tf_op jit(solution)/shard_map/ppermute | solution.py:319
  121.9 1.6 %shard_map.144.refs_0_ = f32[3,64,128]{2,1,0:T(8,128)} custom-call(f32[3,64,128]{2,1,0:T(8,128)} %get-tuple-element.21.next_ref, bf16[3,64,128]{2,1,0:T(8,128)(2,1)} %get-tuple-element.25.refs_0_, bf16[3,64,128]{2,1,0:T(8,128)(2,1)} %copy-done.14, bf16[3,64,128]{2,1,0:T(8,128)(2,1)} %copy-done.16, bf16[3,64,128]{2,1,0:T(8,128)(2,1)} %copy-done.18), custom_call_target="tpu_custom_call" | custom-call | tf_op jit(solution)/shard_map/pallas_call | solution.py:449
  123.5 1.1 collective-permute-start.13
  124.6 2.4 %collective-permute-start.14 = (f32[3,64,128]{2,1,0:T(8,128)}, f32[3,64,128]{2,1,0:T(8,128)S(1)}, u32[]{:S(2)}, u32[]{:S(2)}) collective-permute-start(f32[3,64,128]{2,1,0:T(8,128)} %shard_map.144.refs_0_), channel_id=1, source_target_pairs={{0,2},{1,3},{2,0},{3,1},{4,6},{5,7},{6,4},{7,5},{8,10},{9,11},{10,... | collective-permute-start | bytes 294920 | tf_op jit(solution)/shard_map/ppermute | solution.py:319
  127.4 3.3 %collective-permute-done.13.refs_1_ = f32[3,64,128]{2,1,0:T(8,128)S(1)} collective-permute-done((f32[3,64,128]{2,1,0:T(8,128)}, f32[3,64,128]{2,1,0:T(8,128)S(1)}, u32[]{:S(2)}, u32[]{:S(2)}) %collective-permute-start.13) | collective-permute-done | bytes 98336 | tf_op jit(solution)/shard_map/ppermute | solution.py:319
  130.7 2.8 %collective-permute-done.14.refs_2_ = f32[3,64,128]{2,1,0:T(8,128)S(1)} collective-permute-done((f32[3,64,128]{2,1,0:T(8,128)}, f32[3,64,128]{2,1,0:T(8,128)S(1)}, u32[]{:S(2)}, u32[]{:S(2)}) %collective-permute-start.14) | collective-permute-done | bytes 98336 | tf_op jit(solution)/shard_map/ppermute | solution.py:319
  133.5 0.6 copy-done.7
  134.1 0.6 copy-done.8
  134.7 1.8 %shard_map.145 = f32[3,256,128]{2,1,0:T(8,128)} custom-call(s32[1]{0:T(128)} %bitcast.place_ref, f32[3,64,128]{2,1,0:T(8,128)} %shard_map.144.refs_0_, f32[3,64,128]{2,1,0:T(8,128)} %copy-done.6, f32[3,64,128]{2,1,0:T(8,128)} %copy-done.7, f32[3,64,128]{2,1,0:T(8,128)} %copy-done.8), custom_call_target="tpu_custom_call" | custom-call | tf_op jit(solution)/shard_map/pallas_call | solution.py:451
  136.5 2.1 %copy.24 = f32[1,3,256,128]{3,1,2,0:T(4,128)} copy(f32[1,3,256,128]{3,2,1,0:T(8,128)} %bitcast.26) | data formatting | bytes 786432
  (45 shorter events, 3.7 us)
Async XLA Ops:
  1.8 47.3 %copy-start = (f32[3,32768]{1,0:T(4,128)S(1)}, f32[3,32768]{1,0:T(4,128)}, u32[]{:S(2)}) copy-start(f32[3,32768]{1,0:T(4,128)} %param.15) | copy-start | bytes 1179652
  3.7 7.8 %collective-permute-start = (bf16[384,256]{1,0:T(8,128)(2,1)}, bf16[384,256]{1,0:T(8,128)(2,1)S(1)}, u32[]{:S(2)}, u32[]{:S(2)}) collective-permute-start(bf16[384,256]{1,0:T(8,128)(2,1)} %shard_map.136.own_ref), channel_id=1, source_target_pairs={{0,4},{4,8},{8,12},{12,16},{16,20},{20,24},{24,28},{1,5},{5,9},{9,... | collective-permute-start | bytes 589832 | tf_op jit(solution)/shard_map/ppermute | solution.py:319
  6.1 5.6 %collective-permute-start.1 = (bf16[384,256]{1,0:T(8,128)(2,1)}, bf16[384,256]{1,0:T(8,128)(2,1)S(1)}, u32[]{:S(2)}, u32[]{:S(2)}) collective-permute-start(bf16[384,256]{1,0:T(8,128)(2,1)} %shard_map.136.own_ref), channel_id=1, source_target_pairs={{4,0},{8,4},{12,8},{16,12},{20,16},{24,20},{28,24},{5,1},{9,5},{13... | collective-permute-start | bytes 589832 | tf_op jit(solution)/shard_map/ppermute | solution.py:319
  11.5 73.8 %copy-start.12 = (f32[32,3,128]{2,0,1:T(8,128)S(1)}, f32[32,3,128]{2,0,1:T(8,128)}, u32[]{:S(2)}) copy-start(f32[32,3,128]{2,0,1:T(8,128)} %param.26) | copy-start | bytes 147460
  11.5 0.7 copy-start.2
  12.2 0.7 copy-start.3
  32.5 7.5 %collective-permute-start.2 = (bf16[3,256,128]{2,1,0:T(8,128)(2,1)S(1)}, bf16[3,256,128]{2,1,0:T(8,128)(2,1)S(1)}, u32[]{:S(2)}, u32[]{:S(2)}) collective-permute-start(bf16[3,256,128]{2,1,0:T(8,128)(2,1)S(1)} %get-tuple-element.30), channel_id=1, source_target_pairs={{4,0},{8,4},{12,8},{16,12},{20,16},{24,20},{28,24},{5,1},{9,5},{13... | collective-permute-start | bytes 589832 | tf_op jit(solution)/shard_map/ppermute | solution.py:319
  33.8 7.3 %collective-permute-start.3 = (bf16[3,256,128]{2,1,0:T(8,128)(2,1)S(1)}, bf16[3,256,128]{2,1,0:T(8,128)(2,1)S(1)}, u32[]{:S(2)}, u32[]{:S(2)}) collective-permute-start(bf16[3,256,128]{2,1,0:T(8,128)(2,1)S(1)} %get-tuple-element.29), channel_id=1, source_target_pairs={{0,4},{4,8},{8,12},{12,16},{16,20},{20,24},{24,28},{1,5},{5,9},{9,... | collective-permute-start | bytes 589832 | tf_op jit(solution)/shard_map/ppermute | solution.py:319
  40.0 1.0 copy-start.4
  41.1 0.7 copy-start.5
  43.6 6.3 %collective-permute-start.4 = (bf16[3,64,128]{2,1,0:T(8,128)(2,1)}, bf16[3,64,128]{2,1,0:T(8,128)(2,1)S(1)}, u32[]{:S(2)}, u32[]{:S(2)}) collective-permute-start(bf16[3,64,128]{2,1,0:T(8,128)(2,1)} %get-tuple-element.18), channel_id=1, source_target_pairs={{0,1},{1,2},{2,3},{3,0},{4,5},{5,6},{6,7},{7,4},{8,9},{9,10},{10,1... | collective-permute-start | bytes 147464 | tf_op jit(solution)/shard_map/ppermute | solution.py:319
  45.2 5.2 %collective-permute-start.5 = (bf16[3,64,128]{2,1,0:T(8,128)(2,1)}, bf16[3,64,128]{2,1,0:T(8,128)(2,1)S(1)}, u32[]{:S(2)}, u32[]{:S(2)}) collective-permute-start(bf16[3,64,128]{2,1,0:T(8,128)(2,1)} %get-tuple-element.19), channel_id=1, source_target_pairs={{0,2},{1,3},{2,0},{3,1},{4,6},{5,7},{6,4},{7,5},{8,10},{9,11},{10,... | collective-permute-start | bytes 147464 | tf_op jit(solution)/shard_map/ppermute | solution.py:319
  47.7 5.4 %collective-permute-start.6 = (bf16[3,64,128]{2,1,0:T(8,128)(2,1)}, bf16[3,64,128]{2,1,0:T(8,128)(2,1)S(1)}, u32[]{:S(2)}, u32[]{:S(2)}) collective-permute-start(bf16[3,64,128]{2,1,0:T(8,128)(2,1)} %get-tuple-element.20), channel_id=1, source_target_pairs={{0,3},{1,0},{2,1},{3,2},{4,7},{5,4},{6,5},{7,6},{8,11},{9,8},{10,9... | collective-permute-start | bytes 147464 | tf_op jit(solution)/shard_map/ppermute | solution.py:319
  49.9 3.2 %copy-start.9 = (bf16[3,64,128]{2,1,0:T(8,128)(2,1)}, bf16[3,64,128]{2,1,0:T(8,128)(2,1)S(1)}, u32[]{:S(2)}) copy-start(bf16[3,64,128]{2,1,0:T(8,128)(2,1)S(1)} %collective-permute-done.4.refs_1_) | copy-start | bytes 147460
  50.4 2.8 %copy-start.10 = (bf16[3,64,128]{2,1,0:T(8,128)(2,1)}, bf16[3,64,128]{2,1,0:T(8,128)(2,1)S(1)}, u32[]{:S(2)}) copy-start(bf16[3,64,128]{2,1,0:T(8,128)(2,1)S(1)} %collective-permute-done.5.refs_2_) | copy-start | bytes 147460
  53.1 0.6 copy-start.11
  55.6 20.1 %collective-permute-start.7 = (bf16[3,64,128]{2,1,0:T(8,128)(2,1)}, bf16[3,64,128]{2,1,0:T(8,128)(2,1)S(1)}, u32[]{:S(2)}, u32[]{:S(2)}) collective-permute-start(bf16[3,64,128]{2,1,0:T(8,128)(2,1)} %get-tuple-element.24.refs_0_), channel_id=1, source_target_pairs={{0,1},{1,2},{2,3},{3,0},{4,5},{5,6},{6,7},{7,4},{8,9},{9,10},{10,1... | collective-permute-start | bytes 147464 | tf_op jit(solution)/shard_map/ppermute | solution.py:319
  55.7 20.0 %collective-permute-start.8 = (bf16[3,64,128]{2,1,0:T(8,128)(2,1)}, bf16[3,64,128]{2,1,0:T(8,128)(2,1)S(1)}, u32[]{:S(2)}, u32[]{:S(2)}) collective-permute-start(bf16[3,64,128]{2,1,0:T(8,128)(2,1)} %get-tuple-element.24.refs_0_), channel_id=1, source_target_pairs={{0,2},{1,3},{2,0},{3,1},{4,6},{5,7},{6,4},{7,5},{8,10},{9,11},{10,... | collective-permute-start | bytes 147464 | tf_op jit(solution)/shard_map/ppermute | solution.py:319
  58.3 17.4 %collective-permute-start.9 = (bf16[3,64,128]{2,1,0:T(8,128)(2,1)}, bf16[3,64,128]{2,1,0:T(8,128)(2,1)S(1)}, u32[]{:S(2)}, u32[]{:S(2)}) collective-permute-start(bf16[3,64,128]{2,1,0:T(8,128)(2,1)} %get-tuple-element.24.refs_0_), channel_id=1, source_target_pairs={{0,3},{1,0},{2,1},{3,2},{4,7},{5,4},{6,5},{7,6},{8,11},{9,8},{10,9... | collective-permute-start | bytes 147464 | tf_op jit(solution)/shard_map/ppermute | solution.py:319
  75.7 0.6 copy-start.13
  75.7 0.6 copy-start.15
  76.3 0.6 copy-start.17
  81.9 8.3 %all-to-all-start.1 = ((bf16[8,16,256]{2,1,0:T(8,128)(2,1)}), bf16[8,16,256]{2,1,0:T(8,128)(2,1)S(1)}, u32[]{:S(2)}, u32[]{:S(2)}) async-start(bf16[8,16,256]{2,1,0:T(8,128)(2,1)} %shard_map.141), calls=%async_computation.1 | async-start | bytes 131072 | tf_op jit(solution)/shard_map/all_to_all | solution.py:415
  90.2 0.6 copy-start.1
  113.1 6.2 %collective-permute-start.10 = (bf16[3,64,128]{2,1,0:T(8,128)(2,1)}, bf16[3,64,128]{2,1,0:T(8,128)(2,1)S(1)}, u32[]{:S(2)}, u32[]{:S(2)}) collective-permute-start(bf16[3,64,128]{2,1,0:T(8,128)(2,1)} %get-tuple-element.26), channel_id=1, source_target_pairs={{0,1},{1,2},{2,3},{3,0},{4,5},{5,6},{6,7},{7,4},{8,9},{9,10},{10,1... | collective-permute-start | bytes 147464 | tf_op jit(solution)/shard_map/ppermute | solution.py:319
  115.0 6.2 %collective-permute-start.11 = (bf16[3,64,128]{2,1,0:T(8,128)(2,1)}, bf16[3,64,128]{2,1,0:T(8,128)(2,1)S(1)}, u32[]{:S(2)}, u32[]{:S(2)}) collective-permute-start(bf16[3,64,128]{2,1,0:T(8,128)(2,1)} %get-tuple-element.27), channel_id=1, source_target_pairs={{0,2},{1,3},{2,0},{3,1},{4,6},{5,7},{6,4},{7,5},{8,10},{9,11},{10,... | collective-permute-start | bytes 147464 | tf_op jit(solution)/shard_map/ppermute | solution.py:319
  115.1 6.1 %collective-permute-start.12 = (bf16[3,64,128]{2,1,0:T(8,128)(2,1)}, bf16[3,64,128]{2,1,0:T(8,128)(2,1)S(1)}, u32[]{:S(2)}, u32[]{:S(2)}) collective-permute-start(bf16[3,64,128]{2,1,0:T(8,128)(2,1)} %get-tuple-element.28), channel_id=1, source_target_pairs={{0,3},{1,0},{2,1},{3,2},{4,7},{5,4},{6,5},{7,6},{8,11},{9,8},{10,9... | collective-permute-start | bytes 147464 | tf_op jit(solution)/shard_map/ppermute | solution.py:319
  119.4 1.9 %copy-start.14 = (bf16[3,64,128]{2,1,0:T(8,128)(2,1)}, bf16[3,64,128]{2,1,0:T(8,128)(2,1)S(1)}, u32[]{:S(2)}) copy-start(bf16[3,64,128]{2,1,0:T(8,128)(2,1)S(1)} %collective-permute-done.10.refs_1_) | copy-start | bytes 147460
  121.3 0.6 copy-start.16
  121.3 0.6 copy-start.18
  123.5 7.2 %collective-permute-start.13 = (f32[3,64,128]{2,1,0:T(8,128)}, f32[3,64,128]{2,1,0:T(8,128)S(1)}, u32[]{:S(2)}, u32[]{:S(2)}) collective-permute-start(f32[3,64,128]{2,1,0:T(8,128)} %shard_map.144.refs_0_), channel_id=1, source_target_pairs={{0,1},{1,2},{2,3},{3,0},{4,5},{5,6},{6,7},{7,4},{8,9},{9,10},{10,1... | collective-permute-start | bytes 294920 | tf_op jit(solution)/shard_map/ppermute | solution.py:319
  124.6 8.8 %collective-permute-start.14 = (f32[3,64,128]{2,1,0:T(8,128)}, f32[3,64,128]{2,1,0:T(8,128)S(1)}, u32[]{:S(2)}, u32[]{:S(2)}) collective-permute-start(f32[3,64,128]{2,1,0:T(8,128)} %shard_map.144.refs_0_), channel_id=1, source_target_pairs={{0,2},{1,3},{2,0},{3,1},{4,6},{5,7},{6,4},{7,5},{8,10},{9,11},{10,... | collective-permute-start | bytes 294920 | tf_op jit(solution)/shard_map/ppermute | solution.py:319
  127.0 6.5 %collective-permute-start.15 = (f32[3,64,128]{2,1,0:T(8,128)}, f32[3,64,128]{2,1,0:T(8,128)S(1)}, u32[]{:S(2)}, u32[]{:S(2)}) collective-permute-start(f32[3,64,128]{2,1,0:T(8,128)} %shard_map.144.refs_0_), channel_id=1, source_target_pairs={{0,3},{1,0},{2,1},{3,2},{4,7},{5,4},{6,5},{7,6},{8,11},{9,8},{10,9... | collective-permute-start | bytes 294920 | tf_op jit(solution)/shard_map/ppermute | solution.py:319
  130.7 2.8 %copy-start.6 = (f32[3,64,128]{2,1,0:T(8,128)}, f32[3,64,128]{2,1,0:T(8,128)S(1)}, u32[]{:S(2)}) copy-start(f32[3,64,128]{2,1,0:T(8,128)S(1)} %collective-permute-done.13.refs_1_) | copy-start | bytes 294916
  133.5 0.6 copy-start.7
  134.1 0.6 copy-start.8

commit v2 on v1

v2 whole, which is shorter than its diff:
```python
import functools

import jax
import jax.numpy as jnp
from jax import lax
from jax.experimental import pallas as pl
from jax.experimental.pallas import tpu as pltpu
from jax.sharding import PartitionSpec as P

CAP = 4
LANES = 128
GROUP_CELLS = 8
CHUNK = 256
EACH = 8
BF = jnp.bfloat16
F32 = jnp.float32
VMEM = pl.BlockSpec(memory_space=pltpu.VMEM)
SMEM = pl.BlockSpec(memory_space=pltpu.SMEM)
PARAMS = pltpu.CompilerParams(vmem_limit_bytes=32 * 1024 * 1024)
NT = (((1,), (1,)), ((), ()))
NN = (((1,), (0,)), ((), ()))


def pinned(array):
    return pltpu.with_memory_space_constraint(array, pltpu.VMEM)


def call(kernel, outs, in_specs, out_specs=None, **extra):
    many = isinstance(outs, tuple)
    specs = out_specs if out_specs is not None else ((VMEM,) * len(outs) if many else VMEM)
    run = pl.pallas_call(
        kernel,
        out_shape=outs,
        in_specs=in_specs,
        out_specs=specs,
        compiler_params=PARAMS,
        **extra,
    )

    def placed(*arrays):
        return run(
            *(
                pinned(array) if spec is VMEM else array
                for array, spec in zip(arrays, in_specs, strict=True)
            )
        )

    return placed


def shape_of(dims, dtype):
    return pltpu.VMEM(dims, dtype)


def dot(left, right, dims=NN):
    return lax.dot_general(left, right, dims, preferred_element_type=F32)


def one_hot(rows, line):
    places = lax.broadcasted_iota(jnp.int32, (rows, line.shape[1]), 0).astype(jnp.int16)
    return jnp.where(places == line.astype(jnp.int16), jnp.ones((), BF), jnp.zeros((), BF))


def chosen(picked, low):
    spots = lax.broadcasted_iota(jnp.int32, (8, low.shape[1]), 0)
    kept = [None] * 3
    for start in range(0, LANES, 8):
        mask = spots == low - start
        for part in range(3):
            piece = picked[part * LANES + start : part * LANES + start + 8]
            rest = 0.0 if kept[part] is None else kept[part]
            kept[part] = jnp.where(mask, piece, rest)
    return [jnp.sum(each, axis=0, keepdims=True) for each in kept]


def spread_rows(lines, low):
    spots = lax.broadcasted_iota(jnp.int32, (LANES, low.shape[1]), 0).astype(jnp.int16)
    mask = spots == low.astype(jnp.int16)
    return jnp.concatenate(
        [
            jnp.where(mask, jnp.broadcast_to(line.astype(BF), mask.shape), jnp.zeros((), BF))
            for line in lines
        ],
        axis=0,
    )


def front_kernel(slabs, owner_ref, now_ref, nodes_ref, table_ref, request_ref, slot_ref):
    for part in range(3):
        table_ref[pl.ds(part * LANES, LANES), :] = now_ref[:, part, :].T.astype(BF)
    request_ref[...] = jnp.zeros_like(request_ref)

    def step(block, counts):
        owner = owner_ref[block]
        rank = jnp.int32(0)
        for slab in range(slabs):
            rank = jnp.where(owner == slab, counts[slab], rank)
        slot_ref[block] = owner * CAP + rank
        request_ref[owner, pl.ds(rank, 1), :] = nodes_ref[pl.ds(block, 1), :]
        return tuple(counts[slab] + (owner == slab).astype(jnp.int32) for slab in range(slabs))

    lax.fori_loop(0, nodes_ref.shape[0], step, (jnp.int32(0),) * slabs)


def stress_of(full, shear, bulk):
    cofactor = [
        [
            full[(a + 1) % 3][(b + 1) % 3] * full[(a + 2) % 3][(b + 2) % 3]
            - full[(a + 1) % 3][(b + 2) % 3] * full[(a + 2) % 3][(b + 1) % 3]
            for b in range(3)
        ]
        for a in range(3)
    ]
    volume = (
        full[0][0] * cofactor[0][0] + full[0][1] * cofactor[0][1] + full[0][2] * cofactor[0][2]
    )
    clamped = jnp.maximum(volume, 0.3)
    factor = (bulk * jnp.log(clamped) - shear) / clamped
    return [[shear * full[a][b] + factor * cofactor[a][b] for b in range(3)] for a in range(3)]


def cell_kernel(
    low_ref, own_ref, high_ref, nodes_ref, grads_ref, weights_ref, shear_ref, bulk_ref,
    down_ref, stay_ref, up_ref, total_ref, table_ref,
):
    cells, _, support, points = grads_ref.shape
    rows = own_ref.shape[1]
    each = GROUP_CELLS
    count = each * support
    for place, ref in enumerate((low_ref, own_ref, high_ref)):
        table_ref[:, place * rows : (place + 1) * rows] = ref[...]
    cell_mask = (
        lax.broadcasted_iota(jnp.int32, (each, count), 1) // support
        == lax.broadcasted_iota(jnp.int32, (each, count), 0)
    )
    spot = lax.broadcasted_iota(jnp.int32, (each, 1), 0)
    for base in range(0, cells, each):
        nodes = jnp.concatenate(
            [nodes_ref[base + cell : base + cell + 1, :] for cell in range(each)], axis=1
        )
        high, low = nodes >> 7, nodes & (LANES - 1)
        found = [[], [], []]
        for start in range(0, count, CHUNK):
            part = slice(start, start + CHUNK)
            picked = dot(table_ref[...], one_hot(3 * rows, high[:, part]))
            for held, line in zip(found, chosen(picked, low[:, part])):
                held.append(line)
        left = jnp.concatenate(
            [jnp.where(cell_mask, jnp.concatenate(held, axis=1), 0.0) for held in found], axis=0
        ).astype(BF)
        slopes = [grads_ref[base : base + each, axis].reshape(count, points) for axis in range(3)]
        grad = [dot(left, slopes[axis]) for axis in range(3)]
        full = [
            [grad[b][a * each : (a + 1) * each] + (1.0 if a == b else 0.0) for b in range(3)]
            for a in range(3)
        ]
        shear = jnp.zeros((each, 1), F32)
        bulk = jnp.zeros((each, 1), F32)
        for cell in range(each):
            shear = jnp.where(spot == cell, shear_ref[base + cell], shear)
            bulk = jnp.where(spot == cell, bulk_ref[base + cell], bulk)
        stress = stress_of(full, shear, bulk)
        weights = weights_ref[base : base + each, :]
        back = None
        for axis in range(3):
            wide = jnp.concatenate([weights * stress[a][axis] for a in range(3)], axis=0)
            term = dot(wide.astype(BF), slopes[axis], NT)
            back = term if back is None else back + term
        lines = [
            jnp.sum(
                jnp.where(cell_mask, back[a * each : (a + 1) * each], 0.0), axis=0, keepdims=True
            )
            for a in range(3)
        ]
        term = dot(spread_rows(lines, low), one_hot(3 * rows, high), NT)
        total_ref[...] = term if base == 0 else total_ref[...] + term
    for part in range(3):
        plane = total_ref[pl.ds(part * LANES, LANES), :]
        for place, ref in enumerate((down_ref, stay_ref, up_ref)):
            ref[part] = plane[:, place * rows : (place + 1) * rows].T.astype(BF)


def combine_kernel(quarters, place_ref, own_ref, up_ref, down_ref, *outs):
    depth = own_ref.shape[1] // quarters
    for shift in range(quarters):
        first = lax.rem(place_ref[0] + shift, quarters) * depth
        window = pl.ds(pl.multiple_of(first, depth), depth)
        for part in range(3):
            outs[shift][part] = (
                own_ref[part, window, :].astype(F32)
                + up_ref[part, window, :].astype(F32)
                + down_ref[part, window, :].astype(F32)
            ).astype(BF)


def advance_kernel(
    quarters, place_ref, now_ref, prev_ref, mass_ref, *refs
):
    parts, next_ref, send_ref = refs[:quarters], refs[quarters], refs[quarters + 1]
    depth = next_ref.shape[1]
    window = pl.ds(pl.multiple_of(place_ref[0] * depth, depth), depth)
    mass = mass_ref[window, :]
    for part in range(3):
        force = parts[0][part].astype(F32)
        for other in parts[1:]:
            force = force + other[part].astype(F32)
        value = 2.0 * now_ref[window, part, :] - prev_ref[window, part, :] - mass * force
        next_ref[part] = value
        send_ref[part] = value.astype(BF)


def lookup_kernel(quarters, slabs, place_ref, asked_ref, *refs):
    parts, out_ref, table_ref = refs[:quarters], refs[quarters], refs[quarters + 1]
    depth = parts[0].shape[1]
    gathered = refs[quarters + 2]
    for shift in range(quarters):
        owner = lax.rem(place_ref[0] - shift + quarters, quarters)
        window = pl.ds(pl.multiple_of(owner * depth, depth), depth)
        for part in range(3):
            gathered[part, window, :] = parts[shift][part].astype(F32)
    rows = depth * quarters
    for part in range(3):
        table_ref[pl.ds(part * LANES, LANES), :] = gathered[part].T.astype(BF)
    support = asked_ref.shape[2]
    pad = jnp.zeros((out_ref.shape[1] - 3 * CAP, support), F32)

    def step(slab, carry):
        lines = asked_ref[slab]
        found = [[], [], []]
        for slot in range(CAP):
            line = lines[slot : slot + 1]
            picked = dot(table_ref[...], one_hot(rows, line >> 7))
            for held, each in zip(found, chosen(picked, line & (LANES - 1))):
                held.append(each)
        out_ref[slab] = jnp.concatenate(found[0] + found[1] + found[2] + [pad], axis=0).astype(BF)
        return carry

    lax.fori_loop(0, slabs, step, 0, unroll=4)


def block_kernel(
    slot_ref, values_ref, phi_ref, corr_ref, target_ref, fixed_ref, out_ref, hold, sent
):
    slabs, height, support = values_ref.shape
    blocks = phi_ref.shape[0]
    for slab in range(slabs):
        hold[slab] = values_ref[slab].astype(F32)
    sent[...] = jnp.zeros_like(sent)
    pad = jnp.zeros((5, support), F32)

    def step(turn, carry):
        places, phis, works = [], [], []
        for local in range(EACH):
            block = turn * EACH + local
            slot = slot_ref[block]
            slab, rank = slot // CAP, lax.rem(slot, CAP)
            places.append((block, slab, rank))
            works.append(
                jnp.concatenate(
                    [hold[slab, pl.ds(part * CAP + rank, 1), :] for part in range(3)] + [pad],
                    axis=0,
                ).astype(BF)
            )
            phis.append(phi_ref[block].astype(BF))
        works = [dot(work, phi, NT) for work, phi in zip(works, phis)]
        resids = []
        for (block, _, _), interp in zip(places, works):
            goal = jnp.concatenate(
                [target_ref[block], jnp.zeros((5, interp.shape[1]), F32)], axis=0
            )
            fixed = fixed_ref[pl.ds(block, 1), :].astype(F32)
            resids.append((fixed * (goal - interp)).astype(BF))
        works = [
            dot(resid, corr_ref[block].astype(BF), NT)
            for (block, _, _), resid in zip(places, resids)
        ]
        works = [dot(corr.astype(BF), phi) for corr, phi in zip(works, phis)]
        for (_, slab, rank), delta in zip(places, works):
            for part in range(3):
                sent[slab, pl.ds(part * CAP + rank, 1), :] = delta[part : part + 1]
        return carry

    lax.fori_loop(0, blocks // EACH, step, 0)
    for slab in range(slabs):
        out_ref[slab] = sent[slab].astype(BF)


def spread_kernel(quarters, slabs, place_ref, asked_ref, arrived_ref, *refs):
    outs, total_ref = refs[:quarters], refs[quarters]
    depth = outs[0].shape[1]
    rows = depth * quarters
    for slab in range(slabs):
        lines = asked_ref[slab]
        values = arrived_ref[slab].astype(F32)
        wide, hots = [], []
        for slot in range(CAP):
            line = lines[slot : slot + 1]
            picks = [values[part * CAP + slot : part * CAP + slot + 1] for part in range(3)]
            wide.append(spread_rows(picks, line & (LANES - 1)))
            hots.append(one_hot(rows, line >> 7))
        term = dot(jnp.concatenate(wide, axis=1), jnp.concatenate(hots, axis=1), NT)
        total_ref[...] = term if slab == 0 else total_ref[...] + term
    natural = refs[quarters + 1]
    for part in range(3):
        natural[part] = total_ref[pl.ds(part * LANES, LANES), :].T
    for shift in range(quarters):
        first = lax.rem(place_ref[0] + shift, quarters) * depth
        window = pl.ds(pl.multiple_of(first, depth), depth)
        for part in range(3):
            outs[shift][part] = natural[part, window, :].astype(BF)


def finish_kernel(next_ref, *refs):
    out_ref = refs[-1]
    for part in range(3):
        value = refs[0][part].astype(F32)
        for other in refs[1:-1]:
            value = value + other[part].astype(F32)
        out_ref[part] = (next_ref[part] + value).astype(BF)


def gather_kernel(quarters, place_ref, *refs):
    parts, out_ref = refs[:quarters], refs[quarters]
    depth = parts[0].shape[1]
    for shift in range(quarters):
        owner = lax.rem(place_ref[0] - shift + quarters, quarters)
        window = pl.ds(pl.multiple_of(owner * depth, depth), depth)
        for part in range(3):
            out_ref[window, part, :] = parts[shift][part].astype(F32)


def shifted(array, axis, by, wrap):
    size = lax.axis_size(axis)
    if wrap:
        pairs = [(i, (i + by) % size) for i in range(size)]
    else:
        pairs = [(i, i + by) for i in range(size) if 0 <= i + by < size]
    return lax.ppermute(array, axis, pairs)


def body(
    disp_now,
    disp_prev,
    inv_mass,
    cell_nodes,
    shape_grads,
    cell_weights,
    cell_shear,
    cell_bulk,
    block_owner,
    block_nodes,
    block_phi,
    block_corr,
    block_target,
    block_fixed,
):
    width = disp_now.shape[1]
    slabs = lax.axis_size("slab")
    quarters = lax.axis_size("group")
    rows = width // LANES
    depth = rows // quarters
    place = lax.axis_index("group").astype(jnp.int32).reshape(1)
    now = jnp.transpose(disp_now.reshape(3, rows, LANES), (1, 0, 2))
    prev = jnp.transpose(disp_prev.reshape(3, rows, LANES), (1, 0, 2))
    mass = inv_mass.reshape(rows, LANES)
    blocks, support = block_nodes.shape

    own, request, slot = call(
        functools.partial(front_kernel, slabs),
        (
            shape_of((3 * LANES, rows), BF),
            shape_of((slabs, CAP, support), jnp.int32),
            jax.ShapeDtypeStruct((blocks,), jnp.int32),
        ),
        [SMEM, VMEM, VMEM],
        (VMEM, VMEM, SMEM),
    )(block_owner.reshape(blocks), now, block_nodes)
    low = shifted(own, "slab", 1, False)
    high = shifted(own, "slab", -1, False)
    asked = lax.all_to_all(request, "slab", split_axis=0, concat_axis=0, tiled=True)

    down, stay, up = call(
        cell_kernel,
        (shape_of((3, rows, LANES), BF),) * 3,
        [VMEM] * 6 + [SMEM] * 2,
        scratch_shapes=[
            pltpu.VMEM((3 * LANES, 3 * rows), F32),
            pltpu.VMEM((3 * LANES, 3 * rows), BF),
        ],
    )(low, own, high, cell_nodes, shape_grads, cell_weights, cell_shear, cell_bulk)

    from_above = shifted(down, "slab", -1, False)
    from_below = shifted(up, "slab", 1, False)
    quarter = (3, depth, LANES)
    pieces = call(
        functools.partial(combine_kernel, quarters),
        (shape_of(quarter, BF),) * quarters,
        [SMEM] + [VMEM] * 3,
    )(place, stay, from_above, from_below)
    pieces = [pieces[0]] + [
        shifted(pieces[by], "group", by, True) for by in range(1, quarters)
    ]
    mine, sent = call(
        functools.partial(advance_kernel, quarters),
        (shape_of(quarter, F32), shape_of(quarter, BF)),
        [SMEM] + [VMEM] * (3 + quarters),
    )(place, now, prev, mass, *pieces)
    tables = [sent] + [shifted(sent, "group", by, True) for by in range(1, quarters)]
    height = -(-3 * CAP // 16) * 16
    looked = call(
        functools.partial(lookup_kernel, quarters, slabs),
        shape_of((slabs, height, support), BF),
        [SMEM] + [VMEM] * (1 + quarters),
        scratch_shapes=[
            pltpu.VMEM((3 * LANES, rows), BF),
            pltpu.VMEM((3, rows, LANES), F32),
        ],
    )(place, asked, *tables)
    values = lax.all_to_all(looked, "slab", split_axis=0, concat_axis=0, tiled=True)

    outgoing = call(
        block_kernel,
        shape_of((slabs, height, support), BF),
        [SMEM] + [VMEM] * 5,
        scratch_shapes=[
            pltpu.VMEM((slabs, height, support), F32),
            pltpu.VMEM((slabs, height, support), F32),
        ],
    )(slot, values, block_phi, block_corr, block_target, block_fixed)
    arrived = lax.all_to_all(outgoing, "slab", split_axis=0, concat_axis=0, tiled=True)
    added = call(
        functools.partial(spread_kernel, quarters, slabs),
        (shape_of(quarter, BF),) * quarters,
        [SMEM] + [VMEM] * 2,
        scratch_shapes=[
            pltpu.VMEM((3 * LANES, rows), F32),
            pltpu.VMEM((3, rows, LANES), F32),
        ],
    )(place, asked, arrived)
    added = [added[0]] + [shifted(added[by], "group", by, True) for by in range(1, quarters)]
    final = call(finish_kernel, shape_of(quarter, BF), [VMEM] * (1 + quarters))(mine, *added)
    finals = [final] + [shifted(final, "group", by, True) for by in range(1, quarters)]
    whole = call(
        functools.partial(gather_kernel, quarters),
        shape_of((rows, 3, LANES), F32),
        [SMEM] + [VMEM] * quarters,
    )(place, *finals)
    return jnp.transpose(whole, (1, 0, 2)).reshape(3, width)


def solution(mesh):
    placed = (
        P(None, "slab"),
        P(None, "slab"),
        P("slab"),
        P(("slab", "group"), None),
        P(("slab", "group"), None, None, None),
        P(("slab", "group"), None),
        P(("slab", "group")),
        P(("slab", "group")),
        P(("slab", "group"), None),
        P(("slab", "group"), None),
        P(("slab", "group"), None, None),
        P(("slab", "group"), None, None),
        P(("slab", "group"), None, None),
        P(("slab", "group"), None),
    )
    return jax.shard_map(
        body, mesh=mesh, in_specs=placed, out_specs=P(None, "slab"), check_vma=False
    )
```

time: 140 us -> 113 us (0.81)
  Pallas kernels: 47.2 us -> 23.8 us
  local copies, waits for them, and re-layouts: 18.2 us -> 13.5 us
  blocking collectives: 22.3 us -> 20.9 us
    pallas_call x10 -> x9, Pallas kernels: 47.2 us -> 23.8 us  [placed(): run(*(pinned(array) if spec is VMEM else array for array, spec in zip(arr...]
    reshape x4 -> x0, local copies, waits for them, and re-layouts: 4.88 us -> none  [the longest x1 1.45 us: body(): lines = cell_nodes.reshape(steps, 1, GROUP_CELLS * count)]
    unnamed x42 -> x36, local copies, waits for them, and re-layouts: 11.5 us -> 13.5 us
    squeeze x1 -> x0, local copies, waits for them, and re-layouts: 1.83 us -> none  [body(): from_below = shifted(partial[2], 'slab', 1, False)]
    all_to_all x1, blocking collectives: 8.97 us -> 7.4 us  [body(): lax.all_to_all(outgoing, 'slab', split_axis=0, concat_axis=0, tiled=True)]
    ppermute x16, waiting for transfers between devices: 13.7 us -> 15.1 us  [shifted(): return lax.ppermute(array, axis, pairs)]
  transfers between devices with their start and end apart: 17 -> 17, of which waited for: 9 -> 11; matrix products, arithmetic and copies ran while one was open for 5% -> 1% of each run, Pallas kernels for 2% -> 0%
where the time goes in v2:
time: 113 us; the launch traced here: 112 us
  starting transfers between devices  34.1 us (30%)
  Pallas kernels  23.8 us (21%)
  blocking collectives  20.9 us (18%)
  waiting for transfers between devices  19.2 us (17%)
  local copies, waits for them, and re-layouts  13.5 us (12%)
    ppermute x16, starting transfers between devices, shifted(): return lax.ppermute(array, axis, pairs)  30.8 us
    pallas_call x9, Pallas kernels, placed(): run(*(pinned(array) if spec is VMEM else array for array, spec in zip(arr...  23.8 us
    ppermute x16, waiting for transfers between devices, shifted(): return lax.ppermute(array, axis, pairs)  15.1 us
    all_to_all x1, blocking collectives, body(): lax.all_to_all(request, 'slab', split_axis=0, concat_axis=0, tiled=True)  13.5 us
    unnamed x36, local copies, waits for them, and re-layouts  13.5 us
    all_to_all x1, blocking collectives, body(): lax.all_to_all(outgoing, 'slab', split_axis=0, concat_axis=0, tiled=True)  7.4 us
    all_to_all x1, waiting for transfers between devices, body(): lax.all_to_all(looked, 'slab', split_axis=0, concat_axis=0, tiled=True)  4.11 us
    all_to_all x1, starting transfers between devices, body(): lax.all_to_all(looked, 'slab', split_axis=0, concat_axis=0, tiled=True)  3.35 us
  transfers between devices with their start and end apart: 17, of which 11 were waited for; matrix products, arithmetic and copies ran while one was open for 1% of the time, Pallas kernels for 0%

profile of v2, /device:TPU:0, one launch (start us, length us, event | category | flops | bytes accessed | tf_op | source)
XLA Modules:
  0.0 111.7 jit_solution(4864320778669276756)
XLA Ops:
  0.0 1.0 copy-done.3
  1.0 0.8 copy-done.8
  1.8 0.7 copy-done.12
  2.5 2.1 %shard_map.136 = (bf16[384,256]{1,0:T(8,128)(2,1)S(1)}, s32[8,4,256]{2,1,0:T(4,128)S(1)}, s32[32]{0:T(128)S(1)}) custom-call(s32[32]{0:T(128)S(1)} %bitcast.17, f32[256,3,128]{2,1,0:T(4,128)S(1)} %bitcast.13, s32[32,256]{1,0:T(8,128)S(1)} %copy-done.8), custom_call_target="tpu_custom_call" | custom-call | tf_op jit(solution)/shard_map/pallas_call | solution.py:41
  4.6 0.5 copy-done.15
  5.1 2.4 %collective-permute-start = (bf16[384,256]{1,0:T(8,128)(2,1)S(1)}, bf16[384,256]{1,0:T(8,128)(2,1)S(1)}, u32[]{:S(2)}, u32[]{:S(2)}) collective-permute-start(bf16[384,256]{1,0:T(8,128)(2,1)S(1)} %get-tuple-element.21.own_ref), channel_id=1, source_target_pairs={{0,4},{4,8},{8,12},{12,16},{16,20},{20,24},{24,28},{1,5},{5,9},{9,... | collective-permute-start | bytes 589832 | tf_op jit(solution)/shard_map/ppermute | solution.py:338
  7.5 1.3 %collective-permute-start.1 = (bf16[384,256]{1,0:T(8,128)(2,1)S(1)}, bf16[384,256]{1,0:T(8,128)(2,1)S(1)}, u32[]{:S(2)}, u32[]{:S(2)}) collective-permute-start(bf16[384,256]{1,0:T(8,128)(2,1)S(1)} %get-tuple-element.21.own_ref), channel_id=1, source_target_pairs={{4,0},{8,4},{12,8},{16,12},{20,16},{24,20},{28,24},{5,1},{9,5},{13... | collective-permute-start | bytes 589832 | tf_op jit(solution)/shard_map/ppermute | solution.py:338
  8.8 4.1 %collective-permute-done.1.high_ref = bf16[384,256]{1,0:T(8,128)(2,1)S(1)} collective-permute-done((bf16[384,256]{1,0:T(8,128)(2,1)S(1)}, bf16[384,256]{1,0:T(8,128)(2,1)S(1)}, u32[]{:S(2)}, u32[]{:S(2)}) %collective-permute-start.1) | collective-permute-done | bytes 196640 | tf_op jit(solution)/shard_map/ppermute | solution.py:338
  13.0 2.3 %copy-done = bf16[32,3,192,128]{3,2,1,0:T(8,128)(2,1)S(1)} copy-done((bf16[32,3,192,128]{3,2,1,0:T(8,128)(2,1)S(1)}, bf16[32,3,192,128]{3,2,1,0:T(8,128)(2,1)}, u32[]{:S(2)}) %copy-start) | copy-done | bytes 4718616
  15.3 0.8 copy-done.7
  16.1 0.7 copy-done.10
  16.8 0.7 copy-done.13
  17.4 0.7 copy-done.14
  18.1 12.7 %shard_map.137 = (bf16[3,256,128]{2,1,0:T(8,128)(2,1)}, bf16[3,256,128]{2,1,0:T(8,128)(2,1)S(1)}, bf16[3,256,128]{2,1,0:T(8,128)(2,1)}) custom-call(bf16[384,256]{1,0:T(8,128)(2,1)S(1)} %collective-permute-done.low_ref, bf16[384,256]{1,0:T(8,128)(2,1)S(1)} %get-tuple-element.21.own_ref, bf16[384,256]{1,0:T(8,128)(2,1)S(1)} %collective-permute-done.1.high_ref, ...), custom_call_target="tpu_custom_call" | custom-call | tf_op jit(solution)/shard_map/pallas_call | solution.py:41
  30.8 1.3 %collective-permute-start.2 = (bf16[3,256,128]{2,1,0:T(8,128)(2,1)}, bf16[3,256,128]{2,1,0:T(8,128)(2,1)S(1)}, u32[]{:S(2)}, u32[]{:S(2)}) collective-permute-start(bf16[3,256,128]{2,1,0:T(8,128)(2,1)} %get-tuple-element.23), channel_id=1, source_target_pairs={{4,0},{8,4},{12,8},{16,12},{20,16},{24,20},{28,24},{5,1},{9,5},{13... | collective-permute-start | bytes 589832 | tf_op jit(solution)/shard_map/ppermute | solution.py:338
  32.1 7.4 %collective-permute-start.3 = (bf16[3,256,128]{2,1,0:T(8,128)(2,1)}, bf16[3,256,128]{2,1,0:T(8,128)(2,1)}, u32[]{:S(2)}, u32[]{:S(2)}) collective-permute-start(bf16[3,256,128]{2,1,0:T(8,128)(2,1)} %get-tuple-element.24), channel_id=1, source_target_pairs={{0,4},{4,8},{8,12},{12,16},{16,20},{20,24},{24,28},{1,5},{5,9},{9,... | collective-permute-start | bytes 589832 | tf_op jit(solution)/shard_map/ppermute | solution.py:338
  39.5 0.7 collective-permute-done.3.down_ref
  40.2 1.0 shard_map.138
  41.2 1.6 %collective-permute-start.4 = (bf16[3,64,128]{2,1,0:T(8,128)(2,1)S(1)}, bf16[3,64,128]{2,1,0:T(8,128)(2,1)S(1)}, u32[]{:S(2)}, u32[]{:S(2)}) collective-permute-start(bf16[3,64,128]{2,1,0:T(8,128)(2,1)S(1)} %get-tuple-element.26), channel_id=1, source_target_pairs={{0,1},{1,2},{2,3},{3,0},{4,5},{5,6},{6,7},{7,4},{8,9},{9,10},{10,1... | collective-permute-start | bytes 147464 | tf_op jit(solution)/shard_map/ppermute | solution.py:338
  42.8 2.6 %collective-permute-start.5 = (bf16[3,64,128]{2,1,0:T(8,128)(2,1)S(1)}, bf16[3,64,128]{2,1,0:T(8,128)(2,1)S(1)}, u32[]{:S(2)}, u32[]{:S(2)}) collective-permute-start(bf16[3,64,128]{2,1,0:T(8,128)(2,1)S(1)} %get-tuple-element.27), channel_id=1, source_target_pairs={{0,2},{1,3},{2,0},{3,1},{4,6},{5,7},{6,4},{7,5},{8,10},{9,11},{10,... | collective-permute-start | bytes 147464 | tf_op jit(solution)/shard_map/ppermute | solution.py:338
  45.4 1.4 %collective-permute-start.6 = (bf16[3,64,128]{2,1,0:T(8,128)(2,1)S(1)}, bf16[3,64,128]{2,1,0:T(8,128)(2,1)S(1)}, u32[]{:S(2)}, u32[]{:S(2)}) collective-permute-start(bf16[3,64,128]{2,1,0:T(8,128)(2,1)S(1)} %get-tuple-element.28), channel_id=1, source_target_pairs={{0,3},{1,0},{2,1},{3,2},{4,7},{5,4},{6,5},{7,6},{8,11},{9,8},{10,9... | collective-permute-start | bytes 147464 | tf_op jit(solution)/shard_map/ppermute | solution.py:338
  47.1 0.7 collective-permute-done.5.refs_2_
  47.8 2.6 %collective-permute-done.6.refs_3_ = bf16[3,64,128]{2,1,0:T(8,128)(2,1)S(1)} collective-permute-done((bf16[3,64,128]{2,1,0:T(8,128)(2,1)S(1)}, bf16[3,64,128]{2,1,0:T(8,128)(2,1)S(1)}, u32[]{:S(2)}, u32[]{:S(2)}) %collective-permute-start.6) | collective-permute-done | bytes 49184 | tf_op jit(solution)/shard_map/ppermute | solution.py:338
  50.4 0.9 copy-done.6
  51.7 2.6 %collective-permute-start.8 = (bf16[3,64,128]{2,1,0:T(8,128)(2,1)S(1)}, bf16[3,64,128]{2,1,0:T(8,128)(2,1)S(1)}, u32[]{:S(2)}, u32[]{:S(2)}) collective-permute-start(bf16[3,64,128]{2,1,0:T(8,128)(2,1)S(1)} %get-tuple-element.32.refs_0_), channel_id=1, source_target_pairs={{0,2},{1,3},{2,0},{3,1},{4,6},{5,7},{6,4},{7,5},{8,10},{9,11},{10,... | collective-permute-start | bytes 147464 | tf_op jit(solution)/shard_map/ppermute | solution.py:338
  54.4 1.0 collective-permute-start.9
  55.3 13.5 %all_to_all.15.asked_ref = s32[8,4,256]{2,1,0:T(4,128)S(1)} all-to-all(s32[8,4,256]{2,1,0:T(4,128)} %copy-done.9), channel_id=1, replica_groups=mesh['slab'=8,'group'=4] {'slab'}, dimensions={0} | all-to-all | bytes 65536 | tf_op jit(solution)/shard_map/all_to_all | solution.py:380
  68.9 3.1 %shard_map.140 = bf16[8,16,256]{2,1,0:T(8,128)(2,1)} custom-call(s32[1]{0:T(128)} %bitcast.place_ref, s32[8,4,256]{2,1,0:T(4,128)S(1)} %all_to_all.15.asked_ref, bf16[3,64,128]{2,1,0:T(8,128)(2,1)S(1)} %get-tuple-element.32.refs_0_, bf16[3,64,128]{2,1,0:T(8,128)(2,1)S(1)} %collective-permute-done.7.refs_1_, ...), custom_call_target="tpu_custom_call" | custom-call | tf_op jit(solution)/shard_map/pallas_call | solution.py:41
  72.0 3.4 %all-to-all-start.1 = ((bf16[8,16,256]{2,1,0:T(8,128)(2,1)}), bf16[8,16,256]{2,1,0:T(8,128)(2,1)S(1)}, u32[]{:S(2)}, u32[]{:S(2)}) async-start(bf16[8,16,256]{2,1,0:T(8,128)(2,1)} %shard_map.140), calls=%async_computation.1 | async-start | bytes 131072 | tf_op jit(solution)/shard_map/all_to_all | solution.py:419
  75.4 0.8 copy.15.target_ref
  76.2 4.1 %all-to-all-done.1.values_ref = bf16[8,16,256]{2,1,0:T(8,128)(2,1)S(1)} async-done(((bf16[8,16,256]{2,1,0:T(8,128)(2,1)}), bf16[8,16,256]{2,1,0:T(8,128)(2,1)S(1)}, u32[]{:S(2)}, u32[]{:S(2)}) %all-to-all-start.1) | async-done | bytes 65568 | tf_op jit(solution)/shard_map/all_to_all | solution.py:419
  80.3 2.2 %copy-done.1 = f32[32,128,256]{2,1,0:T(8,128)S(1)} copy-done((f32[32,128,256]{2,1,0:T(8,128)S(1)}, f32[32,128,256]{2,1,0:T(8,128)}, u32[]{:S(2)}) %copy-start.1) | copy-done | bytes 4194328
  82.5 0.6 copy-done.16
  83.1 2.6 %shard_map.141 = bf16[8,16,256]{2,1,0:T(8,128)(2,1)S(1)} custom-call(s32[32]{0:T(128)S(1)} %copy-done.16, bf16[8,16,256]{2,1,0:T(8,128)(2,1)S(1)} %all-to-all-done.1.values_ref, f32[32,128,256]{2,1,0:T(8,128)S(1)} %copy-done.1, f32[32,128,128]{2,1,0:T(8,128)S(1)} %copy-done.2, f32[32,3,128]{2,1,0:T(4,128)S(1)} %copy.15.target_ref, s32[32,128]{1,0:T(8,128)S(1)} %copy-done.11), custom_call_target="tpu_custom_call" | custom-call | tf_op jit(solution)/shard_map/pallas_call | solution.py:41
  85.8 7.4 %all_to_all.16.arrived_ref = bf16[8,16,256]{2,1,0:T(8,128)(2,1)S(1)} all-to-all(bf16[8,16,256]{2,1,0:T(8,128)(2,1)S(1)} %shard_map.141), channel_id=1, replica_groups=mesh['slab'=8,'group'=4] {'slab'}, dimensions={0} | all-to-all | bytes 131072 | tf_op jit(solution)/shard_map/all_to_all | solution.py:430
  93.2 1.9 %shard_map.142 = (bf16[3,64,128]{2,1,0:T(8,128)(2,1)S(1)}, bf16[3,64,128]{2,1,0:T(8,128)(2,1)S(1)}, bf16[3,64,128]{2,1,0:T(8,128)(2,1)S(1)}, bf16[3,64,128]{2,1,0:T(8,128)(2,1)S(1)}) custom-call(s32[1]{0:T(128)} %bitcast.place_ref, s32[8,4,256]{2,1,0:T(4,128)S(1)} %all_to_all.15.asked_ref, bf16[8,16,256]{2,1,0:T(8,128)(2,1)S(1)} %all_to_all.16.arrived_ref), custom_call_target="tpu_custom_call" | custom-call | tf_op jit(solution)/shard_map/pallas_call | solution.py:41
  95.1 2.0 %collective-permute-start.10 = (bf16[3,64,128]{2,1,0:T(8,128)(2,1)S(1)}, bf16[3,64,128]{2,1,0:T(8,128)(2,1)S(1)}, u32[]{:S(2)}, u32[]{:S(2)}) collective-permute-start(bf16[3,64,128]{2,1,0:T(8,128)(2,1)S(1)} %get-tuple-element.34), channel_id=1, source_target_pairs={{0,1},{1,2},{2,3},{3,0},{4,5},{5,6},{6,7},{7,4},{8,9},{9,10},{10,1... | collective-permute-start | bytes 147464 | tf_op jit(solution)/shard_map/ppermute | solution.py:338
  97.0 0.5 collective-permute-start.11
  97.5 2.5 %collective-permute-start.12 = (bf16[3,64,128]{2,1,0:T(8,128)(2,1)S(1)}, bf16[3,64,128]{2,1,0:T(8,128)(2,1)S(1)}, u32[]{:S(2)}, u32[]{:S(2)}) collective-permute-start(bf16[3,64,128]{2,1,0:T(8,128)(2,1)S(1)} %get-tuple-element.36), channel_id=1, source_target_pairs={{0,3},{1,0},{2,1},{3,2},{4,7},{5,4},{6,5},{7,6},{8,11},{9,8},{10,9... | collective-permute-start | bytes 147464 | tf_op jit(solution)/shard_map/ppermute | solution.py:338
  100.1 1.1 collective-permute-done.10.refs_1_
  101.2 1.9 %collective-permute-done.11.refs_2_ = bf16[3,64,128]{2,1,0:T(8,128)(2,1)S(1)} collective-permute-done((bf16[3,64,128]{2,1,0:T(8,128)(2,1)S(1)}, bf16[3,64,128]{2,1,0:T(8,128)(2,1)S(1)}, u32[]{:S(2)}, u32[]{:S(2)}) %collective-permute-start.11) | collective-permute-done | bytes 49184 | tf_op jit(solution)/shard_map/ppermute | solution.py:338
  103.1 1.1 %collective-permute-start.13 = (bf16[3,64,128]{2,1,0:T(8,128)(2,1)S(1)}, bf16[3,64,128]{2,1,0:T(8,128)(2,1)S(1)}, u32[]{:S(2)}, u32[]{:S(2)}) collective-permute-start(bf16[3,64,128]{2,1,0:T(8,128)(2,1)S(1)} %shard_map.143.refs_0_), channel_id=1, source_target_pairs={{0,1},{1,2},{2,3},{3,0},{4,5},{5,6},{6,7},{7,4},{8,9},{9,10},{10,1... | collective-permute-start | bytes 147464 | tf_op jit(solution)/shard_map/ppermute | solution.py:338
  104.2 2.4 %collective-permute-start.14 = (bf16[3,64,128]{2,1,0:T(8,128)(2,1)S(1)}, bf16[3,64,128]{2,1,0:T(8,128)(2,1)S(1)}, u32[]{:S(2)}, u32[]{:S(2)}) collective-permute-start(bf16[3,64,128]{2,1,0:T(8,128)(2,1)S(1)} %shard_map.143.refs_0_), channel_id=1, source_target_pairs={{0,2},{1,3},{2,0},{3,1},{4,6},{5,7},{6,4},{7,5},{8,10},{9,11},{10,... | collective-permute-start | bytes 147464 | tf_op jit(solution)/shard_map/ppermute | solution.py:338
  106.6 0.5 collective-permute-start.15
  107.1 2.0 %collective-permute-done.13.refs_1_ = bf16[3,64,128]{2,1,0:T(8,128)(2,1)S(1)} collective-permute-done((bf16[3,64,128]{2,1,0:T(8,128)(2,1)S(1)}, bf16[3,64,128]{2,1,0:T(8,128)(2,1)S(1)}, u32[]{:S(2)}, u32[]{:S(2)}) %collective-permute-start.13) | collective-permute-done | bytes 49184 | tf_op jit(solution)/shard_map/ppermute | solution.py:338
  109.1 1.0 collective-permute-done.14.refs_2_
  110.1 0.6 collective-permute-done.15.refs_3_
  110.9 0.8 copy.16
  (33 shorter events, 1.1 us)
Async XLA Ops:
  0.0 1.0 copy-start.3
  1.0 0.8 copy-start.8
  1.8 0.7 copy-start.12
  2.5 47.9 %copy-start.4 = (f32[3,32768]{1,0:T(4,128)S(1)}, f32[3,32768]{1,0:T(4,128)}, u32[]{:S(2)}) copy-start(f32[3,32768]{1,0:T(4,128)} %param.14) | copy-start | bytes 1179652
  2.5 77.9 %copy-start.11 = (s32[32,128]{1,0:T(8,128)S(1)}, s32[32,128]{1,0:T(8,128)}, u32[]{:S(2)}) copy-start(s32[32,128]{1,0:T(8,128)} %fixed_ref.1) | copy-start | bytes 49156
  4.6 0.5 copy-start.15
  5.1 25.6 %copy-start.9 = (s32[8,4,256]{2,1,0:T(4,128)}, s32[8,4,256]{2,1,0:T(4,128)S(1)}, u32[]{:S(2)}) copy-start(s32[8,4,256]{2,1,0:T(4,128)S(1)} %get-tuple-element.30) | copy-start | bytes 98308
  5.1 3.7 %collective-permute-start = (bf16[384,256]{1,0:T(8,128)(2,1)S(1)}, bf16[384,256]{1,0:T(8,128)(2,1)S(1)}, u32[]{:S(2)}, u32[]{:S(2)}) collective-permute-start(bf16[384,256]{1,0:T(8,128)(2,1)S(1)} %get-tuple-element.21.own_ref), channel_id=1, source_target_pairs={{0,4},{4,8},{8,12},{12,16},{16,20},{20,24},{24,28},{1,5},{5,9},{9,... | collective-permute-start | bytes 589832 | tf_op jit(solution)/shard_map/ppermute | solution.py:338
  7.5 5.4 %collective-permute-start.1 = (bf16[384,256]{1,0:T(8,128)(2,1)S(1)}, bf16[384,256]{1,0:T(8,128)(2,1)S(1)}, u32[]{:S(2)}, u32[]{:S(2)}) collective-permute-start(bf16[384,256]{1,0:T(8,128)(2,1)S(1)} %get-tuple-element.21.own_ref), channel_id=1, source_target_pairs={{4,0},{8,4},{12,8},{16,12},{20,16},{24,20},{28,24},{5,1},{9,5},{13... | collective-permute-start | bytes 589832 | tf_op jit(solution)/shard_map/ppermute | solution.py:338
  13.0 2.3 %copy-start = (bf16[32,3,192,128]{3,2,1,0:T(8,128)(2,1)S(1)}, bf16[32,3,192,128]{3,2,1,0:T(8,128)(2,1)}, u32[]{:S(2)}) copy-start(bf16[32,3,192,128]{3,2,1,0:T(8,128)(2,1)} %grads_ref.1) | copy-start | bytes 14155780
  15.3 0.8 copy-start.7
  16.1 0.7 copy-start.10
  16.8 0.7 copy-start.13
  17.4 0.7 copy-start.14
  18.1 32.3 %copy-start.5 = (f32[3,32768]{1,0:T(4,128)S(1)}, f32[3,32768]{1,0:T(4,128)}, u32[]{:S(2)}) copy-start(f32[3,32768]{1,0:T(4,128)} %param.15) | copy-start | bytes 1179652
  18.1 62.2 %copy-start.2 = (f32[32,128,128]{2,1,0:T(8,128)S(1)}, f32[32,128,128]{2,1,0:T(8,128)}, u32[]{:S(2)}) copy-start(f32[32,128,128]{2,1,0:T(8,128)} %corr_ref.1) | copy-start | bytes 6291460
  30.8 8.7 %collective-permute-start.2 = (bf16[3,256,128]{2,1,0:T(8,128)(2,1)}, bf16[3,256,128]{2,1,0:T(8,128)(2,1)S(1)}, u32[]{:S(2)}, u32[]{:S(2)}) collective-permute-start(bf16[3,256,128]{2,1,0:T(8,128)(2,1)} %get-tuple-element.23), channel_id=1, source_target_pairs={{4,0},{8,4},{12,8},{16,12},{20,16},{24,20},{28,24},{5,1},{9,5},{13... | collective-permute-start | bytes 589832 | tf_op jit(solution)/shard_map/ppermute | solution.py:338
  32.1 8.1 %collective-permute-start.3 = (bf16[3,256,128]{2,1,0:T(8,128)(2,1)}, bf16[3,256,128]{2,1,0:T(8,128)(2,1)}, u32[]{:S(2)}, u32[]{:S(2)}) collective-permute-start(bf16[3,256,128]{2,1,0:T(8,128)(2,1)} %get-tuple-element.24), channel_id=1, source_target_pairs={{0,4},{4,8},{8,12},{12,16},{16,20},{20,24},{24,28},{1,5},{5,9},{9,... | collective-permute-start | bytes 589832 | tf_op jit(solution)/shard_map/ppermute | solution.py:338
  41.2 5.9 %collective-permute-start.4 = (bf16[3,64,128]{2,1,0:T(8,128)(2,1)S(1)}, bf16[3,64,128]{2,1,0:T(8,128)(2,1)S(1)}, u32[]{:S(2)}, u32[]{:S(2)}) collective-permute-start(bf16[3,64,128]{2,1,0:T(8,128)(2,1)S(1)} %get-tuple-element.26), channel_id=1, source_target_pairs={{0,1},{1,2},{2,3},{3,0},{4,5},{5,6},{6,7},{7,4},{8,9},{9,10},{10,1... | collective-permute-start | bytes 147464 | tf_op jit(solution)/shard_map/ppermute | solution.py:338
  42.8 5.0 %collective-permute-start.5 = (bf16[3,64,128]{2,1,0:T(8,128)(2,1)S(1)}, bf16[3,64,128]{2,1,0:T(8,128)(2,1)S(1)}, u32[]{:S(2)}, u32[]{:S(2)}) collective-permute-start(bf16[3,64,128]{2,1,0:T(8,128)(2,1)S(1)} %get-tuple-element.27), channel_id=1, source_target_pairs={{0,2},{1,3},{2,0},{3,1},{4,6},{5,7},{6,4},{7,5},{8,10},{9,11},{10,... | collective-permute-start | bytes 147464 | tf_op jit(solution)/shard_map/ppermute | solution.py:338
  45.4 5.0 %collective-permute-start.6 = (bf16[3,64,128]{2,1,0:T(8,128)(2,1)S(1)}, bf16[3,64,128]{2,1,0:T(8,128)(2,1)S(1)}, u32[]{:S(2)}, u32[]{:S(2)}) collective-permute-start(bf16[3,64,128]{2,1,0:T(8,128)(2,1)S(1)} %get-tuple-element.28), channel_id=1, source_target_pairs={{0,3},{1,0},{2,1},{3,2},{4,7},{5,4},{6,5},{7,6},{8,11},{9,8},{10,9... | collective-permute-start | bytes 147464 | tf_op jit(solution)/shard_map/ppermute | solution.py:338
  50.4 0.9 copy-start.6
  51.5 17.4 %collective-permute-start.7 = (bf16[3,64,128]{2,1,0:T(8,128)(2,1)S(1)}, bf16[3,64,128]{2,1,0:T(8,128)(2,1)S(1)}, u32[]{:S(2)}, u32[]{:S(2)}) collective-permute-start(bf16[3,64,128]{2,1,0:T(8,128)(2,1)S(1)} %get-tuple-element.32.refs_0_), channel_id=1, source_target_pairs={{0,1},{1,2},{2,3},{3,0},{4,5},{5,6},{6,7},{7,4},{8,9},{9,10},{10,1... | collective-permute-start | bytes 147464 | tf_op jit(solution)/shard_map/ppermute | solution.py:338
  51.7 17.1 %collective-permute-start.8 = (bf16[3,64,128]{2,1,0:T(8,128)(2,1)S(1)}, bf16[3,64,128]{2,1,0:T(8,128)(2,1)S(1)}, u32[]{:S(2)}, u32[]{:S(2)}) collective-permute-start(bf16[3,64,128]{2,1,0:T(8,128)(2,1)S(1)} %get-tuple-element.32.refs_0_), channel_id=1, source_target_pairs={{0,2},{1,3},{2,0},{3,1},{4,6},{5,7},{6,4},{7,5},{8,10},{9,11},{10,... | collective-permute-start | bytes 147464 | tf_op jit(solution)/shard_map/ppermute | solution.py:338
  54.4 14.5 %collective-permute-start.9 = (bf16[3,64,128]{2,1,0:T(8,128)(2,1)S(1)}, bf16[3,64,128]{2,1,0:T(8,128)(2,1)S(1)}, u32[]{:S(2)}, u32[]{:S(2)}) collective-permute-start(bf16[3,64,128]{2,1,0:T(8,128)(2,1)S(1)} %get-tuple-element.32.refs_0_), channel_id=1, source_target_pairs={{0,3},{1,0},{2,1},{3,2},{4,7},{5,4},{6,5},{7,6},{8,11},{9,8},{10,9... | collective-permute-start | bytes 147464 | tf_op jit(solution)/shard_map/ppermute | solution.py:338
  72.0 8.3 %all-to-all-start.1 = ((bf16[8,16,256]{2,1,0:T(8,128)(2,1)}), bf16[8,16,256]{2,1,0:T(8,128)(2,1)S(1)}, u32[]{:S(2)}, u32[]{:S(2)}) async-start(bf16[8,16,256]{2,1,0:T(8,128)(2,1)} %shard_map.140), calls=%async_computation.1 | async-start | bytes 131072 | tf_op jit(solution)/shard_map/all_to_all | solution.py:419
  80.3 2.2 %copy-start.1 = (f32[32,128,256]{2,1,0:T(8,128)S(1)}, f32[32,128,256]{2,1,0:T(8,128)}, u32[]{:S(2)}) copy-start(f32[32,128,256]{2,1,0:T(8,128)} %phi_ref.1) | copy-start | bytes 12582916
  82.5 0.6 copy-start.16
  95.1 6.1 %collective-permute-start.10 = (bf16[3,64,128]{2,1,0:T(8,128)(2,1)S(1)}, bf16[3,64,128]{2,1,0:T(8,128)(2,1)S(1)}, u32[]{:S(2)}, u32[]{:S(2)}) collective-permute-start(bf16[3,64,128]{2,1,0:T(8,128)(2,1)S(1)} %get-tuple-element.34), channel_id=1, source_target_pairs={{0,1},{1,2},{2,3},{3,0},{4,5},{5,6},{6,7},{7,4},{8,9},{9,10},{10,1... | collective-permute-start | bytes 147464 | tf_op jit(solution)/shard_map/ppermute | solution.py:338
  97.0 6.0 %collective-permute-start.11 = (bf16[3,64,128]{2,1,0:T(8,128)(2,1)S(1)}, bf16[3,64,128]{2,1,0:T(8,128)(2,1)S(1)}, u32[]{:S(2)}, u32[]{:S(2)}) collective-permute-start(bf16[3,64,128]{2,1,0:T(8,128)(2,1)S(1)} %get-tuple-element.35), channel_id=1, source_target_pairs={{0,2},{1,3},{2,0},{3,1},{4,6},{5,7},{6,4},{7,5},{8,10},{9,11},{10,... | collective-permute-start | bytes 147464 | tf_op jit(solution)/shard_map/ppermute | solution.py:338
  97.5 5.5 %collective-permute-start.12 = (bf16[3,64,128]{2,1,0:T(8,128)(2,1)S(1)}, bf16[3,64,128]{2,1,0:T(8,128)(2,1)S(1)}, u32[]{:S(2)}, u32[]{:S(2)}) collective-permute-start(bf16[3,64,128]{2,1,0:T(8,128)(2,1)S(1)} %get-tuple-element.36), channel_id=1, source_target_pairs={{0,3},{1,0},{2,1},{3,2},{4,7},{5,4},{6,5},{7,6},{8,11},{9,8},{10,9... | collective-permute-start | bytes 147464 | tf_op jit(solution)/shard_map/ppermute | solution.py:338
  103.1 6.0 %collective-permute-start.13 = (bf16[3,64,128]{2,1,0:T(8,128)(2,1)S(1)}, bf16[3,64,128]{2,1,0:T(8,128)(2,1)S(1)}, u32[]{:S(2)}, u32[]{:S(2)}) collective-permute-start(bf16[3,64,128]{2,1,0:T(8,128)(2,1)S(1)} %shard_map.143.refs_0_), channel_id=1, source_target_pairs={{0,1},{1,2},{2,3},{3,0},{4,5},{5,6},{6,7},{7,4},{8,9},{9,10},{10,1... | collective-permute-start | bytes 147464 | tf_op jit(solution)/shard_map/ppermute | solution.py:338
  104.2 5.9 %collective-permute-start.14 = (bf16[3,64,128]{2,1,0:T(8,128)(2,1)S(1)}, bf16[3,64,128]{2,1,0:T(8,128)(2,1)S(1)}, u32[]{:S(2)}, u32[]{:S(2)}) collective-permute-start(bf16[3,64,128]{2,1,0:T(8,128)(2,1)S(1)} %shard_map.143.refs_0_), channel_id=1, source_target_pairs={{0,2},{1,3},{2,0},{3,1},{4,6},{5,7},{6,4},{7,5},{8,10},{9,11},{10,... | collective-permute-start | bytes 147464 | tf_op jit(solution)/shard_map/ppermute | solution.py:338
  106.6 4.1 %collective-permute-start.15 = (bf16[3,64,128]{2,1,0:T(8,128)(2,1)S(1)}, bf16[3,64,128]{2,1,0:T(8,128)(2,1)S(1)}, u32[]{:S(2)}, u32[]{:S(2)}) collective-permute-start(bf16[3,64,128]{2,1,0:T(8,128)(2,1)S(1)} %shard_map.143.refs_0_), channel_id=1, source_target_pairs={{0,3},{1,0},{2,1},{3,2},{4,7},{5,4},{6,5},{7,6},{8,11},{9,8},{10,9... | collective-permute-start | bytes 147464 | tf_op jit(solution)/shard_map/ppermute | solution.py:338
